TPU v7x, 32 devices: a whole 2x2x4 slice. The times are simulated.
32 devices in a mesh: dp: 4 (over z), tensor: 8 (over y, x, core).
Axes of the slice: x: 2, y: 2, z: 4, core: 2. Of those that a mesh axis runs over, the one named last changes fastest.
Arguments:
- block_input: bfloat16 [1, 12544, 512], P(None, ('dp', 'tensor')), may hold values from -6 to 6
- out_cotangent: bfloat16 [1, 12544, 512], P(None, ('dp', 'tensor')), may hold values from -6 to 6
- live_images: int32 [4], P('dp'), may hold values from 4 to 16, as said below
- width_params: bfloat16 [6, 512], P(None, 'dp'), may hold values from -4 to 4
- w_qkv: bfloat16 [512, 1536], P('dp', 'tensor'), may hold values from -0.25 to 0.25
- qv_bias: bfloat16 [2, 8, 64], P(None, 'tensor', 'dp'), may hold values from -3 to 3
- bias_table: float32 [16, 169], P('tensor'), may hold values from -12 to 320
- w_proj: bfloat16 [512, 512], P('tensor', 'dp'), may hold values from -0.75 to 0.75
- fc1_w: bfloat16 [512, 2048], P('dp', 'tensor'), may hold values from -0.25 to 0.25
- fc1_bias: bfloat16 [8, 256], P('tensor', 'dp'), may hold values from -3 to 3
- fc2_w: bfloat16 [2048, 512], P('tensor', 'dp'), may hold values from -0.125 to 0.125
Outputs:
- block_output: bfloat16 [1, 12544, 512], P(None, ('dp', 'tensor'))
- input_grad: float32 [1, 12544, 512], P(None, ('dp', 'tensor'))
- g_width: float32 [6, 512], P(None, 'dp')
- g_qkv: float32 [512, 1536], P('dp', 'tensor')
- g_qv_bias: float32 [2, 8, 64], P(None, 'tensor', 'dp')
- g_table: float32 [16, 169], P('tensor')
- g_proj: float32 [512, 512], P('tensor', 'dp')
- g_fc1: float32 [512, 2048], P('dp', 'tensor')
- g_fc1_bias: float32 [8, 256], P('tensor', 'dp')
- g_fc2: float32 [2048, 512], P('tensor', 'dp')
Inputs may be any that keep to these rules, and one draw needn't show every extreme that they name: Index d of dp has its first live_images[d] images live, counted over its 1 group in order; some index has all 16 images live.
All inputs are finite; a program needn't handle non-finite values.
Results may differ from a plain program's by a relative error of at most 0.014.
Values may be sent and summed in bfloat16 or wider, within the bound.
No kernel may reach another device: no remote copies, remote signals or barrier semaphores. Data moves between devices by JAX's collectives and lax.ppermute only.
A program may use at most 128 MiB of HBM per device.

v0:
```python
import jax
import jax.numpy as jnp
from jax import lax
from jax.sharding import PartitionSpec as P

HEAD = 32
WIN = 7
SIDE = 14
SHIFT = 3
TABLE = 169


EPSILON = 1e-05
MASKED = -100.0


def window_tables():
    per_side = SIDE // WIN
    places = jnp.arange(SIDE)
    region_band = jnp.where(places < SIDE - WIN, 0, jnp.where(places < SIDE - SHIFT, 1, 2))
    region = region_band[:, None] * 3 + region_band[None, :]
    region = (
        region.reshape(per_side, WIN, per_side, WIN)
        .transpose(0, 2, 1, 3)
        .reshape(per_side * per_side, WIN * WIN)
    )
    masking = jnp.where(region[:, :, None] == region[:, None, :], 0.0, MASKED).astype(jnp.float32)
    cell_ids = jnp.arange(WIN * WIN)
    rowpos = cell_ids // WIN
    colpos = cell_ids % WIN
    relative = (rowpos[:, None] - rowpos[None, :] + WIN - 1) * (2 * WIN - 1) + (
        colpos[:, None] - colpos[None, :] + WIN - 1
    )
    return (masking, relative)


def to_windows(grid_cells):
    image_count, features, per_side = (grid_cells.shape[0], grid_cells.shape[-1], SIDE // WIN)
    grid_cells = grid_cells.reshape(image_count, per_side, WIN, per_side, WIN, features).transpose(
        0, 1, 3, 2, 4, 5
    )
    return grid_cells.reshape(image_count * per_side * per_side, WIN * WIN, features)


def from_windows(windows, image_count):
    per_side, features = (SIDE // WIN, windows.shape[-1])
    grid_cells = windows.reshape(image_count, per_side, per_side, WIN, WIN, features).transpose(
        0, 1, 3, 2, 4, 5
    )
    return grid_cells.reshape(image_count, SIDE, SIDE, features)


def rows_to_windows(rows, image_count):
    grid_cells = jnp.roll(
        rows.reshape(image_count, SIDE, SIDE, rows.shape[-1]), (-SHIFT, -SHIFT), axis=(1, 2)
    )
    return to_windows(grid_cells)


def windows_to_rows(windows, image_count):
    grid_cells = jnp.roll(from_windows(windows, image_count), (SHIFT, SHIFT), axis=(1, 2))
    return grid_cells.reshape(image_count * SIDE * SIDE, windows.shape[-1])


def normalize(value):
    row_mean = jnp.mean(value, axis=-1, keepdims=True)
    centred = value - row_mean
    inv_std = lax.rsqrt(jnp.mean(centred * centred, axis=-1, keepdims=True) + EPSILON)
    return (centred * inv_std, inv_std)


def norm_back(grad, x_hat, inv_std):
    return inv_std * (
        grad
        - jnp.mean(grad, axis=-1, keepdims=True)
        - x_hat * jnp.mean(grad * x_hat, axis=-1, keepdims=True)
    )


def gelu_parts(pre_act):
    normal_cdf = 0.5 * (1.0 + lax.erf(pre_act * 0.7071067811865476))
    normal_pdf = jnp.exp(-0.5 * pre_act * pre_act) * 0.3989422804014327
    return (pre_act * normal_cdf, normal_cdf + pre_act * normal_pdf)


def contract_rows(left, right):
    return lax.dot_general(
        left, right, (((0,), (0,)), ((), ())), preferred_element_type=jnp.float32
    )


def times_transposed(left, right):
    return lax.dot_general(
        left, right, (((1,), (1,)), ((), ())), preferred_element_type=jnp.float32
    )


def per_device(
    block_input,
    out_cotangent,
    live_images,
    width_params,
    w_qkv,
    qv_bias,
    bias_table,
    w_proj,
    fc1_w,
    fc1_bias,
    fc2_w,
):
    micro, rows_dev, width = block_input.shape
    tensor_size = lax.axis_size("tensor")
    tokens = rows_dev * tensor_size
    heads_dev = bias_table.shape[0]
    win_cells = WIN * WIN
    per_image = (SIDE // WIN) ** 2
    q_scale = HEAD ** (-0.5)
    masking, relative = window_tables()
    one_hot = (relative.reshape(-1)[None, :] == jnp.arange(TABLE)[:, None]).astype(jnp.float32)
    att_images = tokens // (SIDE * SIDE)
    position = jnp.dot(bias_table, one_hot, precision=lax.Precision.HIGHEST).reshape(
        heads_dev, win_cells, win_cells
    )
    row_image = (lax.axis_index("tensor") * rows_dev + jnp.arange(rows_dev)) // (SIDE * SIDE)
    live_count = live_images[0]
    acc_qkv = None
    acc_qvb = None
    acc_table = None
    acc_proj = None
    acc_fc1 = None
    acc_b1 = None
    acc_fc2 = None
    w_query = lax.all_gather(w_qkv, "dp", axis=0, tiled=True)
    w_out = lax.all_gather(w_proj, "dp", axis=1, tiled=True)
    w_first = lax.all_gather(fc1_w, "dp", axis=0, tiled=True)
    w_second = lax.all_gather(fc2_w, "dp", axis=1, tiled=True)
    vectors = lax.all_gather(width_params, "dp", axis=1, tiled=True)
    qv_terms = lax.all_gather(qv_bias, "dp", axis=2, tiled=True)
    first_bias = lax.all_gather(fc1_bias, "dp", axis=1, tiled=True)
    vectors = vectors.astype(jnp.float32)
    qv_terms = qv_terms.astype(jnp.float32).reshape(2, heads_dev, HEAD)
    first_bias = first_bias.astype(jnp.float32).reshape(-1)
    x_now = block_input[0].astype(jnp.float32)
    x_hat1, inv_std1 = normalize(x_now)
    normed1 = (x_hat1 * vectors[0] + vectors[1]).astype(jnp.bfloat16)
    att_in = lax.all_gather(normed1, "tensor", axis=0, tiled=True)
    qkv_rows = jnp.dot(att_in, w_query, preferred_element_type=jnp.float32).reshape(
        tokens, heads_dev, 3, HEAD
    )
    query = (qkv_rows[:, :, 0] + qv_terms[0]) * q_scale
    value = qkv_rows[:, :, 2] + qv_terms[1]
    packed = jnp.stack([query, qkv_rows[:, :, 1], value], axis=2).astype(jnp.bfloat16)
    windows = rows_to_windows(packed.reshape(tokens, heads_dev * 3 * HEAD), att_images).reshape(
        -1, win_cells, heads_dev, 3, HEAD
    )
    win_count = windows.shape[0]
    q_win = windows[:, :, :, 0]
    k_win = windows[:, :, :, 1]
    v_win = windows[:, :, :, 2]
    scores = jnp.einsum("wihd,wjhd->whij", q_win, k_win, preferred_element_type=jnp.float32)
    scores = (
        scores.reshape(att_images, per_image, heads_dev, win_cells, win_cells)
        + position[None, None]
        + masking[None, :, None]
    ).reshape(win_count, heads_dev, win_cells, win_cells)
    peak = jnp.max(scores, axis=-1, keepdims=True)
    raised = jnp.exp(scores - peak)
    probs = raised / jnp.sum(raised, axis=-1, keepdims=True)
    probs_b = probs.astype(jnp.bfloat16)
    attended = jnp.einsum(
        "whij,wjhd->wihd", probs_b, v_win, preferred_element_type=jnp.float32
    ).astype(jnp.bfloat16)
    heads_out = windows_to_rows(
        attended.reshape(win_count, win_cells, heads_dev * HEAD), att_images
    )
    x_mid = (
        x_now
        + lax.psum_scatter(
            jnp.dot(heads_out, w_out, preferred_element_type=jnp.float32),
            "tensor",
            scatter_dimension=0,
            tiled=True,
        )
        + vectors[4]
    )
    x_hat2, inv_std2 = normalize(x_mid)
    normed2 = (x_hat2 * vectors[2] + vectors[3]).astype(jnp.bfloat16)
    live_rows = (0 + row_image < live_count).astype(jnp.float32)
    grad_y = out_cotangent[0].astype(jnp.float32) * live_rows[:, None]
    grad_yb = grad_y.astype(jnp.bfloat16)
    normed2_all = lax.all_gather(normed2, "tensor", axis=0, tiled=True)
    pre_act = jnp.dot(normed2_all, w_first, preferred_element_type=jnp.float32) + first_bias
    activated, slope = gelu_parts(pre_act)
    activated_b = activated.astype(jnp.bfloat16)
    out_rows = (
        x_mid
        + lax.psum_scatter(
            jnp.dot(activated_b, w_second, preferred_element_type=jnp.float32).astype(jnp.bfloat16),
            "tensor",
            scatter_dimension=0,
            tiled=True,
        ).astype(jnp.float32)
        + vectors[5]
    )
    grad_y_all = lax.all_gather(grad_yb, "tensor", axis=0, tiled=True)
    acc_fc2 = contract_rows(activated_b, grad_y_all)
    grad_pre = times_transposed(grad_y_all, w_second) * slope
    grad_pre_b = grad_pre.astype(jnp.bfloat16)
    acc_fc1 = contract_rows(normed2_all, grad_pre_b)
    acc_b1 = jnp.sum(grad_pre, axis=0)
    grad_n2 = lax.psum_scatter(
        times_transposed(grad_pre_b, w_first), "tensor", scatter_dimension=0, tiled=True
    )
    out_parts = [out_rows.astype(jnp.bfloat16)]
    grad_mid = grad_y + norm_back(grad_n2 * vectors[2], x_hat2, inv_std2)
    grad_mid_b = grad_mid.astype(jnp.bfloat16)
    grad_mid_all = lax.all_gather(grad_mid_b, "tensor", axis=0, tiled=True)
    acc_proj = contract_rows(heads_out, grad_mid_all)
    grad_att = times_transposed(grad_mid_all, w_out).astype(jnp.bfloat16)
    grad_win = rows_to_windows(grad_att, att_images).reshape(win_count, win_cells, heads_dev, HEAD)
    grad_v = jnp.einsum("whij,wihd->wjhd", probs_b, grad_win, preferred_element_type=jnp.float32)
    grad_probs = jnp.einsum("wihd,wjhd->whij", grad_win, v_win, preferred_element_type=jnp.float32)
    grad_s = probs * (grad_probs - jnp.sum(probs * grad_probs, axis=-1, keepdims=True))
    grad_sb = grad_s.astype(jnp.bfloat16)
    grad_q = (
        jnp.einsum("whij,wjhd->wihd", grad_sb, k_win, preferred_element_type=jnp.float32) * q_scale
    )
    grad_k = jnp.einsum("whij,wihd->wjhd", grad_sb, q_win, preferred_element_type=jnp.float32)
    acc_table = jnp.sum(grad_s, axis=0)
    acc_qvb = jnp.stack([jnp.sum(grad_q, axis=(0, 1)), jnp.sum(grad_v, axis=(0, 1))])
    grad_pack = jnp.stack([grad_q, grad_k, grad_v], axis=3).astype(jnp.bfloat16)
    grad_rows = windows_to_rows(
        grad_pack.reshape(win_count, win_cells, heads_dev * 3 * HEAD), att_images
    )
    acc_qkv = contract_rows(att_in, grad_rows)
    grad_n1 = lax.psum_scatter(
        times_transposed(grad_rows, w_query).astype(jnp.bfloat16),
        "tensor",
        scatter_dimension=0,
        tiled=True,
    ).astype(jnp.float32)
    grad_parts = [grad_mid + norm_back(grad_n1 * vectors[0], x_hat1, inv_std1)]
    width_terms = jnp.stack(
        [
            jnp.sum(grad_n1 * x_hat1, axis=0),
            jnp.sum(grad_n1, axis=0),
            jnp.sum(grad_n2 * x_hat2, axis=0),
            jnp.sum(grad_n2, axis=0),
            jnp.sum(grad_mid, axis=0),
            jnp.sum(grad_y, axis=0),
        ]
    )
    width_total = lax.psum(width_terms, "tensor")
    table_terms = jnp.dot(
        acc_table.reshape(heads_dev, -1), one_hot.T, precision=lax.Precision.HIGHEST
    )
    acc_b1 = acc_b1.reshape(1, -1)
    g_qkv, g_proj, g_fc1, g_fc2, g_width, g_qv_bias, g_fc1_bias = (
        lax.psum_scatter(
            acc_qkv.astype(jnp.bfloat16), "dp", scatter_dimension=0, tiled=True
        ).astype(jnp.float32),
        lax.psum_scatter(
            acc_proj.astype(jnp.bfloat16), "dp", scatter_dimension=1, tiled=True
        ).astype(jnp.float32),
        lax.psum_scatter(
            acc_fc1.astype(jnp.bfloat16), "dp", scatter_dimension=0, tiled=True
        ).astype(jnp.float32),
        lax.psum_scatter(
            acc_fc2.astype(jnp.bfloat16), "dp", scatter_dimension=1, tiled=True
        ).astype(jnp.float32),
        lax.psum_scatter(
            width_total.astype(jnp.bfloat16), "dp", scatter_dimension=1, tiled=True
        ).astype(jnp.float32),
        lax.psum_scatter(
            acc_qvb.reshape(2, 1, -1).astype(jnp.bfloat16), "dp", scatter_dimension=2, tiled=True
        ).astype(jnp.float32),
        lax.psum_scatter(acc_b1.astype(jnp.bfloat16), "dp", scatter_dimension=1, tiled=True).astype(
            jnp.float32
        ),
    )
    g_table = lax.psum(table_terms, "dp")
    return (
        jnp.stack(out_parts),
        jnp.stack(grad_parts),
        g_width,
        g_qkv,
        g_qv_bias,
        g_table,
        g_proj,
        g_fc1,
        g_fc1_bias,
        g_fc2,
    )


def solution(mesh):
    placed = (
        P(None, ("dp", "tensor"), None),
        P(None, ("dp", "tensor"), None),
        P("dp"),
        P(None, "dp"),
        P("dp", "tensor"),
        P(None, "tensor", "dp"),
        P("tensor", None),
        P("tensor", "dp"),
        P("dp", "tensor"),
        P("tensor", "dp"),
        P("tensor", "dp"),
    )
    return jax.shard_map(
        per_device,
        mesh=mesh,
        in_specs=placed,
        out_specs=(
            P(None, ("dp", "tensor"), None),
            P(None, ("dp", "tensor"), None),
            P(None, "dp"),
            P("dp", "tensor"),
            P(None, "tensor", "dp"),
            P("tensor", None),
            P("tensor", "dp"),
            P("dp", "tensor"),
            P("tensor", "dp"),
            P("tensor", "dp"),
        ),
        check_vma=False,
    )
```

profile of v0, /device:TPU:0, one launch (start us, length us, event | category | flops | bytes accessed | tf_op | source)
XLA Modules:
  0.0 663.8 jit_solution(1774179218612301472)
XLA Ops:
  7.2 1.1 convert_reduce_fusion.1
  8.4 1.2 fusion.50
  9.7 13.8 %all_gather.33 = bf16[6,512]{1,0:T(8,128)(2,1)S(1)} all-gather(bf16[6,128]{1,0:T(8,128)(2,1)} %param.14), channel_id=1, replica_groups=mesh['dp'=4,'tensor'=8] {'dp'}, dimensions={1}, use_global_device_ids=true | all-gather | bytes 7680 | tf_op jit(solution)/shard_map/all_gather | solution.py:137
  24.0 2.0 fusion.45
  27.2 13.1 %all_gather.36 = bf16[2,1,64]{1,0,2:T(2,128)(2,1)S(1)} all-gather(bf16[2,1,16]{1,0,2:T(2,128)(2,1)S(1)} %copy.75), channel_id=1, replica_groups=mesh['dp'=4,'tensor'=8] {'dp'}, dimensions={2}, use_global_device_ids=true | all-gather | bytes 320 | tf_op jit(solution)/shard_map/all_gather | solution.py:138
  42.0 12.4 %all_gather.37 = bf16[64,512]{1,0:T(8,128)(2,1)S(1)} all-gather(bf16[64,128]{1,0:T(8,128)(2,1)} %param.18), channel_id=1, replica_groups=mesh['dp'=4,'tensor'=8] {'dp'}, dimensions={1}, use_global_device_ids=true | all-gather | bytes 81920 | tf_op jit(solution)/shard_map/all_gather | solution.py:134
  54.4 13.3 %all_gather.35 = bf16[512,192]{0,1:T(8,128)(2,1)S(1)} all-gather(bf16[128,192]{0,1:T(8,128)(2,1)} %param.15), channel_id=1, replica_groups=mesh['dp'=4,'tensor'=8] {'dp'}, dimensions={0}, use_global_device_ids=true | all-gather | bytes 245760 | tf_op jit(solution)/shard_map/all_gather | solution.py:133
  67.8 3.1 fusion.73
  71.4 6.4 copy.76
  77.8 10.3 %convert_element_type.149 = bf16[16,14,14,192]{3,2,1,0:T(8,128)(2,1)S(1)} reshape(bf16[3136,2,3,32]{3,2,1,0:T(4,128)(2,1)} %copy.76) | data formatting | bytes 2408448 | tf_op jit(solution)/shard_map/convert_element_type | solution.py:152
  90.4 1.6 copy.78
  92.0 5.9 reshape_reshape.11
  97.9 16.4 %fusion.69 = (bf16[64,49,2,1,32]{4,3,2,0,1:T(2,128)(2,1)}, bf16[64,49,2,1,32]{4,3,2,0,1:T(2,128)(2,1)}, bf16[64,49,2,1,32]{4,3,2,0,1:T(2,128)(2,1)S(1)}) fusion(bf16[64,49,2,3,32]{4,3,2,0,1:T(4,128)(2,1)} %reshape_reshape.11), kind=kLoop, calls=%fused_computation.147 | loop fusion | bytes 2408448 | tf_op jit(solution)/shard_map/slice | solution.py:157
  114.3 7.4 %copy.116 = bf16[64,49,2,1,32]{1,4,2,0,3:T(8,128)(2,1)} copy(bf16[64,49,2,1,32]{4,3,2,0,1:T(2,128)(2,1)} %get-tuple-element.26) | data formatting | bytes 802816
  121.8 7.4 %copy.115 = bf16[64,49,2,1,32]{1,4,2,0,3:T(8,128)(2,1)} copy(bf16[64,49,2,1,32]{4,3,2,0,1:T(2,128)(2,1)} %get-tuple-element.27) | data formatting | bytes 802816
  129.2 5.9 copy.117
  135.1 2.7 fusion.22
  138.0 1.2 fusion.71
  139.3 1.9 copy-done.3
  141.8 2.9 copy.84
  144.7 1.0 reshape_reshape.12
  146.7 3.7 fusion.74
  150.5 61.0 %reduce-scatter.24.cloned.1.call-done = f32[392,512]{1,0:T(8,128)} async-done(((f32[3136,512]{1,0:T(8,128)}), f32[392,512]{1,0:T(8,128)}) %reduce-scatter.24.cloned.1.call-update) | async-done | bytes 802832 | tf_op jit(solution)/shard_map/reduce_scatter | solution.py:178
  211.5 1.3 fusion.67
  213.1 1.0 add_convert_fusion.1
  217.3 11.7 %all-reduce = bf16[256]{0:T(256)(128)(2,1)S(1)} all-reduce(bf16[256]{0:T(256)(128)(2,1)S(1)} %dynamic-update-slice), channel_id=1, replica_groups=mesh['dp'=4,'tensor'=8] {'dp'}, use_global_device_ids=true, to_apply=%add | all-reduce | flops 256 | bytes 1024
  229.0 13.8 %all_gather.39 = bf16[512,256]{1,0:T(8,128)(2,1)S(1)} all-gather(bf16[128,256]{1,0:T(8,128)(2,1)S(1)} %copy-done.19), channel_id=1, replica_groups=mesh['dp'=4,'tensor'=8] {'dp'}, dimensions={0}, use_global_device_ids=true | all-gather | bytes 327680 | tf_op jit(solution)/shard_map/all_gather | solution.py:135
  242.8 12.8 %all_gather.41 = bf16[256,512]{1,0:T(8,128)(2,1)S(1)} all-gather(bf16[256,128]{1,0:T(8,128)(2,1)S(1)} %copy-done.20), channel_id=1, replica_groups=mesh['dp'=4,'tensor'=8] {'dp'}, dimensions={1}, use_global_device_ids=true | all-gather | bytes 327680 | tf_op jit(solution)/shard_map/all_gather | solution.py:136
  255.6 5.6 multiply_convert_fusion
  261.2 20.3 %all-gather.9.cloned.1.call-done = bf16[3136,512]{1,0:T(8,128)(2,1)} async-done(((bf16[392,512]{1,0:T(8,128)(2,1)}), bf16[3136,512]{1,0:T(8,128)(2,1)}) %all-gather.9.cloned.1.call-update) | async-done | bytes 3211280 | tf_op jit(solution)/shard_map/all_gather | solution.py:205
  281.5 4.4 fusion.72
  285.9 3.7 fusion.59
  289.7 4.1 convolution_convert_fusion.1
  293.9 58.3 %reduce-scatter.28.cloned.1.call-done = f32[392,512]{1,0:T(8,128)} async-done(((f32[3136,512]{1,0:T(8,128)}), f32[392,512]{1,0:T(8,128)}) %reduce-scatter.28.cloned.1.call-update) | async-done | bytes 802832 | tf_op jit(solution)/shard_map/reduce_scatter | solution.py:211
  352.2 2.2 multiply_reduce_fusion.1
  354.4 47.5 %reduce-scatter.26.cloned.1.call-done = bf16[392,512]{1,0:T(8,128)(2,1)} async-done(((bf16[3136,512]{1,0:T(8,128)(2,1)}), bf16[392,512]{1,0:T(8,128)(2,1)}) %reduce-scatter.26.cloned.1.call-update) | async-done | bytes 401424 | tf_op jit(solution)/shard_map/reduce_scatter | solution.py:197
  401.9 3.0 fusion.65
  407.5 3.5 convolution_convert_fusion.5
  411.9 3.8 convolution_convert_fusion.6
  416.0 23.2 %all-gather.11.cloned.1.call-done = bf16[3136,512]{1,0:T(8,128)(2,1)} async-done(((bf16[392,512]{1,0:T(8,128)(2,1)}), bf16[3136,512]{1,0:T(8,128)(2,1)}) %all-gather.11.cloned.1.call-update) | async-done | bytes 3211280 | tf_op jit(solution)/shard_map/all_gather | solution.py:217
  439.2 3.0 convolution_convert_fusion.2
  445.6 3.0 copy.90
  448.6 3.4 bitcast_reduce_fusion
  452.0 1.3 multiply_reduce_fusion
  453.4 1.1 fusion.13
  455.9 1.1 fusion.12
  457.7 8.9 %copy.95 = bf16[64,49,2,3,32]{4,3,2,0,1:T(4,128)(2,1)} copy(bf16[64,49,2,3,32]{1,4,2,0,3:T(8,128)(2,1)S(1)} %pad_maximum_fusion) | data formatting | bytes 2408448 | tf_op jit(solution)/shard_map/stack | solution.py:231
  466.6 12.6 %convert_element_type.166 = bf16[16,2,2,7,7,192]{5,2,1,0,4,3:T(2,128)(2,1)} reshape(bf16[64,49,2,3,32]{4,3,2,0,1:T(4,128)(2,1)} %copy.95) | data formatting | bytes 2408448 | tf_op jit(solution)/shard_map/convert_element_type | solution.py:231
  479.2 1.8 copy.96
  481.8 1.1 slice.166
  484.4 2.0 convolution_convert_fusion.8
  489.1 2.8 convolution_convert_fusion.7
  492.9 2.7 convolution_convert_fusion
  498.7 3.5 reduce-scatter.32.cloned.1.call-done
  502.2 1.5 convert_element_type.177
  504.8 9.4 %psum.15 = f32[2,169]{1,0:T(2,128)} all-reduce(f32[2,169]{1,0:T(2,128)S(1)} %fusion.9), channel_id=1, replica_groups=mesh['dp'=4,'tensor'=8] {'dp'}, use_global_device_ids=true, to_apply=%region_28.29 | all-reduce | flops 338 | bytes 2704 | tf_op jit(solution)/shard_map/psum | solution.py:281
  514.2 8.3 %reduce-scatter.38.cloned.1.call-done = bf16[16,2]{1,0:T(8,128)(2,1)} async-done(((bf16[64,2]{1,0:T(8,128)(2,1)}), bf16[16,2]{1,0:T(8,128)(2,1)}) %reduce-scatter.38.cloned.1.call-update) | async-done | bytes 80
  523.9 18.3 %reduce-scatter.40.cloned.1.call-done = bf16[128,64]{1,0:T(8,128)(2,1)} async-done(((bf16[512,64]{1,0:T(8,128)(2,1)}), bf16[128,64]{1,0:T(8,128)(2,1)}) %reduce-scatter.40.cloned.1.call-update) | async-done | bytes 16400
  543.7 19.0 %reduce-scatter.36.cloned.1.call-done = bf16[128,192]{1,0:T(8,128)(2,1)} async-done(((bf16[512,192]{1,0:T(8,128)(2,1)}), bf16[128,192]{1,0:T(8,128)(2,1)}) %reduce-scatter.36.cloned.1.call-update) | async-done | bytes 49168
  564.2 46.4 %reduce-scatter.30.cloned.1.call-done = bf16[392,512]{1,0:T(8,128)(2,1)} async-done(((bf16[3136,512]{1,0:T(8,128)(2,1)}), bf16[392,512]{1,0:T(8,128)(2,1)}) %reduce-scatter.30.cloned.1.call-update) | async-done | bytes 401424 | tf_op jit(solution)/shard_map/reduce_scatter | solution.py:236
  610.6 1.5 fusion.53
  612.2 22.9 %psum.14 = bf16[6,512]{1,0:T(8,128)(2,1)S(1)} all-reduce(f32[6,512]{1,0:T(8,128)S(1)} %stack.71), channel_id=1, replica_groups=mesh['dp'=4,'tensor'=8] {'tensor'}, use_global_device_ids=true, to_apply=%region_21.22 | all-reduce | flops 3072 | bytes 18432 | tf_op jit(solution)/shard_map/psum | solution.py:253
  635.9 2.2 fusion.49
  638.2 17.4 %reduce-scatter.34.cloned.1.call-done = bf16[128,6]{1,0:T(8,128)(2,1)} async-done(((bf16[512,6]{1,0:T(8,128)(2,1)}), bf16[128,6]{1,0:T(8,128)(2,1)}) %reduce-scatter.34.cloned.1.call-update) | async-done | bytes 1552
  (183 shorter events, 36.5 us)
Async XLA Ops:
  7.2 33.9 %copy-start = (f32[2,169]{1,0:T(2,128)S(1)}, f32[2,169]{1,0:T(2,128)}, u32[]{:S(2)}) copy-start(f32[2,169]{1,0:T(2,128)} %param.17) | copy-start | bytes 4060
  7.2 60.6 %all-gather.5.cloned.1.call-start = ((), (), s32[]{:S(2)}) async-start(), calls=%async_computation.11 | async-start | bytes 3612672 | tf_op jit(solution)/shard_map/all_gather | solution.py:146
  26.0 185.4 %reduce-scatter.24.cloned.1.call-start = ((), (), s32[]{:S(2)}) async-start(), calls=%async_computation.12 | async-start | bytes 7225344 | tf_op jit(solution)/shard_map/reduce_scatter | solution.py:178
  67.7 3.3 copy-start.13
  138.0 3.1 copy-start.17
  139.3 1.9 copy-start.3
  146.7 3.7 copy-start.7
  150.4 61.1 %copy-start.5 = (bf16[1,392,512]{2,1,0:T(8,128)(2,1)S(1)}, bf16[1,392,512]{2,1,0:T(8,128)(2,1)}, u32[]{:S(2)}) copy-start(bf16[1,392,512]{2,1,0:T(8,128)(2,1)} %param.11) | copy-start | bytes 1204228
  150.4 61.1 %copy-start.26 = (f32[1,512]{1,0:T(1,128)S(1)}, f32[1,512]{1,0:T(1,128)}, u32[]{:S(2)}) copy-start(f32[1,512]{1,0:T(1,128)} %get-tuple-element.36) | copy-start | bytes 6148
  150.4 64.4 %copy-start.15 = (bf16[1,392,512]{2,1,0:T(8,128)(2,1)S(1)}, bf16[1,392,512]{2,1,0:T(8,128)(2,1)}, u32[]{:S(2)}) copy-start(bf16[1,392,512]{2,1,0:T(8,128)(2,1)} %param.12) | copy-start | bytes 1204228
  150.4 65.4 %copy-start.28 = (u32[32]{0:T(128)S(1)}, u32[32]{0:T(128)}, u32[]{:S(2)}) copy-start(u32[32]{0:T(128)} %constant.95) | copy-start | bytes 388
  150.4 66.6 %copy-start.27 = (bf16[1,64]{1,0:T(2,128)(2,1)S(1)}, bf16[1,64]{1,0:T(2,128)(2,1)}, u32[]{:S(2)}) copy-start(bf16[1,64]{1,0:T(2,128)(2,1)} %param.20) | copy-start | bytes 388
  150.4 78.5 %copy-start.19 = (bf16[128,256]{1,0:T(8,128)(2,1)S(1)}, bf16[128,256]{1,0:T(8,128)(2,1)}, u32[]{:S(2)}) copy-start(bf16[128,256]{1,0:T(8,128)(2,1)} %param.19) | copy-start | bytes 196612
  150.4 92.4 %copy-start.20 = (bf16[256,128]{1,0:T(8,128)(2,1)S(1)}, bf16[256,128]{1,0:T(8,128)(2,1)}, u32[]{:S(2)}) copy-start(bf16[256,128]{1,0:T(8,128)(2,1)} %param.21) | copy-start | bytes 196612
  150.4 105.1 %all-gather.7.cloned.1.call-start = ((), (), s32[]{:S(2)}) async-start(), calls=%async_computation.13 | async-start | bytes 3612672 | tf_op jit(solution)/shard_map/all_gather | solution.py:191
  214.1 67.4 %all-gather.9.cloned.1.call-start = ((), (), s32[]{:S(2)}) async-start(), calls=%async_computation.15 | async-start | bytes 3612672 | tf_op jit(solution)/shard_map/all_gather | solution.py:205
  215.7 136.5 %reduce-scatter.28.cloned.1.call-start = ((), (), s32[]{:S(2)}) async-start(), calls=%async_computation.16 | async-start | bytes 7225344 | tf_op jit(solution)/shard_map/reduce_scatter | solution.py:211
  289.7 112.2 %reduce-scatter.26.cloned.1.call-start = ((), (), s32[]{:S(2)}) async-start(), calls=%async_computation.14 | async-start | bytes 3612672 | tf_op jit(solution)/shard_map/reduce_scatter | solution.py:197
  293.8 108.1 %copy-start.25 = (f32[1,512]{1,0:T(1,128)S(1)}, f32[1,512]{1,0:T(1,128)}, u32[]{:S(2)}) copy-start(f32[1,512]{1,0:T(1,128)} %get-tuple-element.33) | copy-start | bytes 6148
  293.8 145.4 %all-gather.11.cloned.1.call-start = ((), (), s32[]{:S(2)}) async-start(), calls=%async_computation.17 | async-start | bytes 3612672 | tf_op jit(solution)/shard_map/all_gather | solution.py:217
  404.9 0.9 copy-start.10
  406.6 89.0 %reduce-scatter.42.cloned.1.call-start = ((), (), s32[]{:S(2)}) async-start(), calls=%async_computation.24 | async-start | bytes 81920
  407.4 89.6 %reduce-scatter.44.cloned.1.call-start = ((), (), s32[]{:S(2)}) async-start(), calls=%async_computation.25 | async-start | bytes 327680
  411.8 90.4 %reduce-scatter.32.cloned.1.call-start = ((), (), s32[]{:S(2)}) async-start(), calls=%async_computation.19 | async-start | bytes 327680 | tf_op jit(solution)/shard_map/reduce_scatter | solution.py:265
  415.7 106.8 %reduce-scatter.38.cloned.1.call-start = ((), (), s32[]{:S(2)}) async-start(), calls=%async_computation.22 | async-start | bytes 20480
  448.6 3.4 copy-start.4
  448.6 3.4 copy-start.18
  453.4 1.2 copy-start.8
  454.7 1.2 copy-start.9
  479.2 5.1 copy-start.2
  484.0 58.2 %reduce-scatter.40.cloned.1.call-start = ((), (), s32[]{:S(2)}) async-start(), calls=%async_computation.23 | async-start | bytes 163840
  484.4 2.0 copy-start.12
  484.4 2.0 copy-start.16
  489.0 3.8 copy-start.14
  489.0 73.6 %reduce-scatter.36.cloned.1.call-start = ((), (), s32[]{:S(2)}) async-start(), calls=%async_computation.21 | async-start | bytes 327680
  492.8 117.8 %reduce-scatter.30.cloned.1.call-start = ((), (), s32[]{:S(2)}) async-start(), calls=%async_computation.18 | async-start | bytes 3612672 | tf_op jit(solution)/shard_map/reduce_scatter | solution.py:236
  495.5 115.1 %copy-start.6 = (bf16[1,392,512]{2,1,0:T(8,128)(2,1)S(1)}, bf16[1,392,512]{2,1,0:T(8,128)(2,1)}, u32[]{:S(2)}) copy-start(bf16[1,392,512]{2,1,0:T(8,128)(2,1)} %param.11) | copy-start | bytes 1204228
  495.5 116.6 %copy-start.21 = (f32[512]{0:T(512)S(1)}, f32[512]{0:T(512)}, u32[]{:S(2)}) copy-start(f32[512]{0:T(512)} %get-tuple-element.10) | copy-start | bytes 6148
  495.5 116.7 %copy-start.22 = (f32[512]{0:T(512)S(1)}, f32[512]{0:T(512)}, u32[]{:S(2)}) copy-start(f32[512]{0:T(512)} %get-tuple-element.15) | copy-start | bytes 6148
  495.5 116.7 %copy-start.23 = (f32[512]{0:T(512)S(1)}, f32[512]{0:T(512)}, u32[]{:S(2)}) copy-start(f32[512]{0:T(512)} %get-tuple-element.20) | copy-start | bytes 6148
  495.5 116.7 %copy-start.24 = (f32[512]{0:T(512)S(1)}, f32[512]{0:T(512)}, u32[]{:S(2)}) copy-start(f32[512]{0:T(512)} %get-tuple-element.32) | copy-start | bytes 6148
  495.5 140.4 %copy-start.11 = (f32[392,512]{1,0:T(8,128)S(1)}, f32[392,512]{1,0:T(8,128)}, u32[]{:S(2)}) copy-start(f32[392,512]{1,0:T(8,128)} %copy-done.10) | copy-start | bytes 2408452
  495.6 161.4 %copy-start.1 = (f32[2,169]{1,0:T(2,128)S(1)}, f32[2,169]{1,0:T(2,128)}, u32[]{:S(2)}) copy-start(f32[2,169]{1,0:T(2,128)} %param.17) | copy-start | bytes 4060
  495.6 160.0 %reduce-scatter.34.cloned.1.call-start = ((), (), s32[]{:S(2)}) async-start(), calls=%async_computation.20 | async-start | bytes 163840
Sparse Core Ops, SparseCore 0:
  26.1 32.1 all-gather.4
  150.5 60.9 reduce-scatter.23
  214.2 32.4 all-gather.6
  249.0 32.4 all-gather.8
  289.8 62.3 reduce-scatter.27
  355.5 46.3 reduce-scatter.25
  406.8 32.4 all-gather.10
  442.0 19.2 reduce-scatter.41
  463.6 18.1 reduce-scatter.43
  483.9 18.2 reduce-scatter.31
  505.0 17.4 reduce-scatter.37
  524.6 17.5 reduce-scatter.39
  544.5 18.1 reduce-scatter.35
  565.9 44.6 reduce-scatter.29
  636.1 19.4 reduce-scatter.33
where the time goes:
time: 668 us; the launch traced here: 664 us
  waiting for transfers between devices  323 us (48%)
  blocking collectives  123 us (18%)
  local copies, waits for them, and re-layouts  117 us (18%)
  matrix products  53.8 us (8%)
  other arithmetic  29.3 us (4%)
  between operations  16.3 us (2%)
    unnamed x21, waiting for transfers between devices  63.1 us
    reduce_scatter x1, waiting for transfers between devices, per_device(): lax.psum_scatter(jnp.dot(heads_out, w_out, preferred_element_type=jnp.flo...  61 us
    reduce_scatter x1, waiting for transfers between devices, per_device(): lax.psum_scatter(times_transposed(grad_pre_b, w_first), 'tensor', scatter...  58.3 us
    reduce_scatter x1, waiting for transfers between devices, per_device(): lax.psum_scatter(jnp.dot(activated_b, w_second, preferred_element_type=jn...  47.5 us
    reduce_scatter x1, waiting for transfers between devices, per_device(): lax.psum_scatter(times_transposed(grad_rows, w_query).astype(jnp.bfloat16...  46.4 us
    unnamed x79, local copies, waits for them, and re-layouts  35.7 us
    all_gather x1, waiting for transfers between devices, per_device(): grad_mid_all = lax.all_gather(grad_mid_b, 'tensor', axis=0, tiled=True)  23.2 us
    psum x1, blocking collectives, per_device(): width_total = lax.psum(width_terms, 'tensor')  22.9 us
  transfers between devices with their start and end apart: 15, of which 11 were waited for; matrix products, arithmetic and copies ran while one was open for 14% of the time, Pallas kernels for 0%

commit v1 on v0

v1 whole, which is shorter than its diff:
```python
import functools

import jax
import jax.numpy as jnp
import numpy as np
from jax import lax
from jax.experimental import pallas as pl
from jax.experimental.pallas import tpu as pltpu
from jax.sharding import PartitionSpec as P

HEAD = 32
WIN = 7
SIDE = 14
SHIFT = 3
TABLE = 169
EPSILON = 1e-05
MASKED = -100.0
NEVER = -1e30
SPAN = 2 * WIN - 1
CELL = 8
SLOT = 64
PAIR = 128
LANES = 128
SMALL = 32
F32 = jnp.float32
BF16 = jnp.bfloat16
AXES = ("dp", "tensor")


def window_constants(images):
    per_side = SIDE // WIN
    place = np.zeros((images * per_side * per_side * SLOT, images * SIDE * SIDE), np.float32)
    band = np.where(np.arange(SIDE) < SIDE - WIN, 0, np.where(np.arange(SIDE) < SIDE - SHIFT, 1, 2))
    mask = np.zeros((per_side, SLOT, PAIR), np.float32)
    select = np.zeros((LANES, PAIR), np.float32)
    region = np.full((per_side, per_side, SLOT), -1)
    for u in range(per_side):
        for v in range(per_side):
            for a in range(WIN):
                for b in range(WIN):
                    r, c = u * WIN + a, v * WIN + b
                    region[u, v, a * CELL + b] = band[r] * 3 + band[c]
                    source = ((r + SHIFT) % SIDE) * SIDE + (c + SHIFT) % SIDE
                    for image in range(images):
                        row = (image * per_side * per_side + u * per_side + v) * SLOT
                        place[row + a * CELL + b, image * SIDE * SIDE + source] = 1
                    select[a * SPAN + b, v * SLOT + a * CELL + b] = 1
    for u in range(per_side):
        for v in range(per_side):
            keys, queries = region[u, v][:, None], region[u, v][None, :]
            both = np.where((keys == queries) | (queries < 0), 0.0, MASKED)
            mask[u, :, v * SLOT : (v + 1) * SLOT] = np.where(keys < 0, NEVER, both)
    return place, mask, select


def dot(a, b):
    return lax.dot_general(a, b, (((1,), (0,)), ((), ())), preferred_element_type=F32)


def dot_nt(a, b):
    return lax.dot_general(a, b, (((1,), (1,)), ((), ())), preferred_element_type=F32)


def split3(value):
    high = value.astype(BF16)
    rest = value - high.astype(F32)
    middle = rest.astype(BF16)
    low = (rest - middle.astype(F32)).astype(BF16)
    return high, middle, low


def half_slot(t, me_t, tensor):
    rel = t ^ me_t
    colour = t & 1
    one, two = (rel >> 1) & 1, (rel >> 2) & 1
    first = one * (1 - colour) + two * colour
    return (rel >> 3) + (tensor // 8) * (first + 2 * (one + two - first))


def each_block(n_dp, tensor, own, other, body):
    me_d, me_t = lax.axis_index("dp"), lax.axis_index("tensor")
    for far, source in ((1, other), (0, own)):

        def step(k, carry, far=far, source=source):
            t = 2 * k + (far ^ (me_t & 1))
            start = n_dp * half_slot(t, me_t, tensor)
            body(far, source, t, [start + (d ^ me_d) for d in range(n_dp)], start)
            return carry

        lax.fori_loop(0, tensor // 2, step, 0)


def normalize(value):
    mean = jnp.mean(value, axis=-1, keepdims=True)
    centred = value - mean
    inv_std = lax.rsqrt(jnp.mean(centred * centred, axis=-1, keepdims=True) + EPSILON)
    return centred * inv_std, inv_std


def norm_back(grad, x_hat, inv_std):
    return inv_std * (
        grad
        - jnp.mean(grad, axis=-1, keepdims=True)
        - x_hat * jnp.mean(grad * x_hat, axis=-1, keepdims=True)
    )


def gelu_parts(pre_act):
    normal_cdf = 0.5 * (1.0 + lax.erf(pre_act * 0.7071067811865476))
    normal_pdf = jnp.exp(-0.5 * pre_act * pre_act) * 0.3989422804014327
    return pre_act * normal_cdf, normal_cdf + pre_act * normal_pdf


def head_masks(dtype):
    lane = lax.broadcasted_iota(jnp.int32, (1, 2 * LANES), 1)
    return [(((lane & (LANES - 1)) >> 5) == h).astype(F32).astype(dtype) for h in range(4)]


def stack_heads(pair, masks):
    both = jnp.concatenate([pair[:SLOT], pair[SLOT:]], axis=1)
    return jnp.concatenate([both * m for m in masks], axis=0)


def block_diag(pair):
    zero = jnp.zeros((SLOT, LANES), pair.dtype)
    return jnp.concatenate(
        [
            jnp.concatenate([pair[:SLOT], zero], axis=1),
            jnp.concatenate([zero, pair[SLOT:]], axis=1),
        ],
        axis=0,
    )


def pick(value):
    return jnp.concatenate([value[:SLOT, :LANES], value[SLOT:, LANES:]], axis=0)


def fold(value, masks):
    total = value[:SLOT] * masks[0]
    for h in range(1, 4):
        total = total + value[h * SLOT : (h + 1) * SLOT] * masks[h]
    return jnp.concatenate([total[:, :LANES], total[:, LANES:]], axis=0)


def identity():
    row = lax.broadcasted_iota(jnp.int32, (LANES, LANES), 0)
    column = lax.broadcasted_iota(jnp.int32, (LANES, LANES), 1)
    return (row == column).astype(F32).astype(BF16)


def pack_kernel(n_dp, tensor, wq, wp, width, qv, table, bias, out, rows):
    columns, lanes = wq.shape[1], wq.shape[0]
    me_d, me_t = lax.axis_index("dp"), lax.axis_index("tensor")
    eye_row = lax.broadcasted_iota(jnp.int32, (columns, columns), 0)
    eye_col = lax.broadcasted_iota(jnp.int32, (columns, columns), 1)
    eye = (eye_row == eye_col).astype(F32).astype(BF16)
    out[0:columns, :] = dot_nt(eye, wq[...]).astype(BF16)
    out[columns : columns + wp.shape[0], :] = wp[...]
    rows[...] = jnp.zeros_like(rows)
    rows[0:6, 0:lanes] = width[...].astype(F32)
    count = qv.shape[2]
    spread = jnp.zeros((8, LANES), F32)
    rows[6:7, 0:count] = qv[0].astype(F32)
    rows[7:8, 0:count] = qv[1].astype(F32)
    begin = lax.rem((me_t * n_dp + me_d) * count, lanes)
    rows[6:8, :] = pltpu.roll(rows[0:8, :], begin, 1)[6:8]
    count = bias.shape[1]
    rows[8:9, 0:count] = bias[...].astype(F32)
    begin = lax.rem((me_t * n_dp + me_d) * count, lanes)
    rows[8:16, :] = pltpu.roll(rows[8:16, :], begin, 1)
    heads, segments = table.shape[0], pl.cdiv(TABLE, lanes)
    for part, piece in enumerate(split3(table[...])):
        for h in range(heads):
            for s in range(segments):
                wide = min(lanes, TABLE - s * lanes)
                row = 9 + (part * heads + h) * segments + s
                rows[row : row + 1, 0:wide] = piece.astype(F32)[
                    h : h + 1, s * lanes : s * lanes + wide
                ]
    out[columns + wp.shape[0] :, :] = rows[:, 0:lanes].astype(BF16)


def forward_kernel(
    n_dp, tensor, x, own, other, place, select, mask,
    n1, q, k, v, wt, vec, probs, att,
    qv_blocks, tab_blocks, tab, spread, position,
):
    width, lanes = x.shape[1], own.shape[2]
    base = own.shape[1] - SMALL
    heads = width // HEAD
    own_heads, segments = heads // tensor, pl.cdiv(TABLE, lanes)
    me_d = lax.axis_index("dp")
    per_tensor, per_both = width // tensor, width // tensor // n_dp

    qv_blocks[...] = jnp.zeros_like(qv_blocks)
    tab_blocks[...] = jnp.zeros_like(tab_blocks)
    spread[...] = jnp.zeros_like(spread)

    def assemble(far, source, t, slots, start):
        for d, s in enumerate(slots):
            for h in range(own_heads):
                for j in range(3):
                    row = pl.multiple_of(j * width + (t * own_heads + h) * HEAD, HEAD)
                    wt[pl.ds(row, HEAD), d * lanes : (d + 1) * lanes] = source[
                        s, (h * 3 + j) * HEAD : (h * 3 + j + 1) * HEAD, :
                    ]
            small = source[s, base : base + SMALL, :].astype(F32)
            block = lax.div(t * per_tensor + d * per_both, lanes)
            qv_blocks[block] = qv_blocks[block] + small[0:8]
        small = source[start, base : base + SMALL, :].astype(F32)
        for h in range(own_heads):
            for s in range(segments):
                rows = [9 + (part * own_heads + h) * segments + s for part in range(3)]
                high, middle, low = [small[r : r + 1] for r in rows]
                tab_blocks[t * own_heads + h, 0:1, s * lanes : (s + 1) * lanes] = high + middle + low

    each_block(n_dp, tensor, own, other, assemble)
    for h in range(heads):
        tab[h : h + 1, :] = tab_blocks[h, 0:1, :]
    for d in range(n_dp):
        small = own[d ^ me_d, base : base + SMALL, :].astype(F32)
        vec[0:8, d * lanes : (d + 1) * lanes] = small[0:8]
    for b in range(width // lanes):
        vec[8:16, b * lanes : (b + 1) * lanes] = qv_blocks[b]

    x_hat, _ = normalize(dot(place[...], x[...]))
    n1[...] = (x_hat * vec[0:1, :] + vec[1:2, :]).astype(BF16)
    scale = HEAD ** (-0.5)
    q[...] = ((dot_nt(n1[...], wt[0:width, :]) + vec[14:15, :]) * scale).astype(BF16)
    k[...] = dot_nt(n1[...], wt[width : 2 * width, :]).astype(BF16)
    v[...] = (dot_nt(n1[...], wt[2 * width :, :]) + vec[15:16, :]).astype(BF16)

    for a in range(WIN):
        for b in range(WIN):
            shift = (SPAN * a + b - (TABLE - 1) // 2) % tab.shape[1]
            spread[:, a * CELL + b, :] = pltpu.roll(tab[...], shift, 1)[:, 0:LANES]
    for g in range(width // LANES):
        rows = spread[4 * g : 4 * g + 4].reshape(4 * SLOT, LANES)
        position[g] = sum(dot(piece, select[...]) for piece in split3(rows))

    masks, eye = head_masks(BF16), identity()

    def window_pair(p, carry):
        rows = pl.ds(pl.multiple_of(p * PAIR, PAIR), PAIR)
        away = mask[p & 1]
        for g in range(width // LANES):
            cols = slice(g * LANES, (g + 1) * LANES)
            scores = dot_nt(stack_heads(k[rows, cols], masks), block_diag(q[rows, cols]))
            scores = (scores + position[g]).reshape(4, SLOT, PAIR) + away[None]
            raised = jnp.exp(scores - jnp.max(scores, axis=1, keepdims=True))
            total = jnp.sum(raised, axis=1, keepdims=True)
            soft = (raised / total).reshape(4 * SLOT, PAIR)
            probs[p, g] = soft
            turned = dot_nt(eye, soft.astype(BF16)).astype(BF16)
            att[rows, cols] = pick(dot(turned, stack_heads(v[rows, cols], masks))).astype(BF16)
        return carry

    lax.fori_loop(0, x_hat.shape[0] // PAIR, window_pair, 0)


def middle_kernel(
    n_dp, tensor, live, x, gy, att, vec, own1, other1, own2, other2, own3, other3, place, back,
    y, g_mid, g_att, f1_send, f1_keep, f2_send, f2_keep, p_send, p_keep, sums, bias_sums,
    wp, n2, n2_t, gyb, gy_t, gn2, y_sum,
):
    width, lanes = x.shape[1], own1.shape[2]
    base = own1.shape[1] - SMALL
    per_tensor = width // tensor
    hidden = own2.shape[2]
    me_t = lax.axis_index("tensor")
    rows = n2.shape[0]
    image_rows = (SIDE // WIN) ** 2 * SLOT

    def assemble(far, source, t, slots, start):
        for d, s in enumerate(slots):
            at = pl.multiple_of(t * per_tensor, per_tensor)
            wp[pl.ds(at, per_tensor), d * lanes : (d + 1) * lanes] = source[
                s, base - per_tensor : base, :
            ]

    each_block(n_dp, tensor, own1, other1, assemble)
    image = me_t * (rows // image_rows) + lax.broadcasted_iota(jnp.int32, (rows, 1), 0) // image_rows
    grad_y = dot(place[...], gy[...]) * (image < live[0]).astype(F32)
    gyb[...] = grad_y.astype(BF16)
    gy_t[...] = grad_y.T.astype(BF16)
    x_mid = dot(place[...], x[...]) + dot(att[...], wp[...]) + vec[4:5, :]
    x_hat, inv_std = normalize(x_mid)
    normed = x_hat * vec[2:3, :] + vec[3:4, :]
    n2[...] = normed.astype(BF16)
    n2_t[...] = normed.T.astype(BF16)
    gn2[...] = jnp.zeros_like(gn2)
    y_sum[...] = x_mid + vec[5:6, :]

    def chunk(far, source, t, slots, start):
        first, second = (other2, other3) if far else (own2, own3)
        f1_out, f2_out = (f1_send, f2_send) if far else (f1_keep, f2_keep)
        f1 = jnp.concatenate([first[s] for s in slots], axis=0)
        f2 = jnp.concatenate([second[s] for s in slots], axis=1)
        bias = []
        for segment in range(hidden // lanes):
            inside = [d for d in range(n_dp) if (d * (hidden // n_dp)) // lanes == segment]
            bias.append(
                sum(source[slots[d], base : base + SMALL, :].astype(F32)[8:9] for d in inside)
            )
        pre_act = dot(n2[...], f1) + jnp.concatenate(bias, axis=1)
        activated, slope = gelu_parts(pre_act)
        activated = activated.astype(BF16)
        y_sum[...] += dot(activated, f2)
        g_f2 = dot(gy_t[...], activated).astype(BF16)
        grad_pre = dot_nt(gyb[...], f2) * slope
        at = pl.multiple_of(t * hidden, hidden)
        bias_sums[0:1, pl.ds(at, hidden)] = jnp.sum(grad_pre, axis=0, keepdims=True)
        grad_pre = grad_pre.astype(BF16)
        gn2[...] += dot_nt(grad_pre, f1)
        g_f1 = dot(n2_t[...], grad_pre).astype(BF16)
        for d, s in enumerate(slots):
            f1_out[s] = g_f1[d * lanes : (d + 1) * lanes]
            f2_out[s] = g_f2[d * lanes : (d + 1) * lanes]

    each_block(n_dp, tensor, own1, other1, chunk)
    y[...] = dot(back[...], y_sum[...].astype(BF16)).astype(BF16)
    grad_n2 = gn2[...]
    grad_mid = grad_y + norm_back(grad_n2 * vec[2:3, :], x_hat, inv_std)
    g_mid[...] = grad_mid
    sums[...] = jnp.zeros_like(sums)
    sums[2:3, :] = jnp.sum(grad_n2 * x_hat, axis=0, keepdims=True)
    sums[3:4, :] = jnp.sum(grad_n2, axis=0, keepdims=True)
    sums[4:5, :] = jnp.sum(grad_mid, axis=0, keepdims=True)
    sums[5:6, :] = jnp.sum(grad_y, axis=0, keepdims=True)
    grad_mid = grad_mid.astype(BF16)
    g_att[...] = dot_nt(grad_mid, wp[...]).astype(BF16)
    wp[...] = dot(att[...].astype(F32).T.astype(BF16), grad_mid).astype(BF16)

    def deal(far, source, t, slots, start):
        out = p_send if far else p_keep
        for d, s in enumerate(slots):
            at = pl.multiple_of(t * per_tensor, per_tensor)
            out[s] = wp[pl.ds(at, per_tensor), d * lanes : (d + 1) * lanes]

    each_block(n_dp, tensor, own1, other1, deal)


def backward_kernel(
    n_dp, tensor, x, n1, q, k, v, probs, wt, vec, g_att, g_mid, sums, bias_sums,
    place, back, select,
    g_x, q_send, q_keep, small,
    g_rows, table_sum, g_w, tab, turned_t,
):
    width, lanes = x.shape[1], q_keep.shape[2]
    heads = width // HEAD
    own_heads, segments = heads // tensor, pl.cdiv(TABLE, lanes)
    hidden = bias_sums.shape[1] // tensor
    groups = width // LANES
    scale = HEAD ** (-0.5)
    masks, masks_f32, eye = head_masks(BF16), head_masks(F32), identity()
    table_sum[...] = jnp.zeros_like(table_sum)
    qv_zero = jnp.zeros((1, width), F32)

    def window_pair(p, carry):
        sum_q, sum_v = carry
        rows = pl.ds(pl.multiple_of(p * PAIR, PAIR), PAIR)
        parts_q, parts_v = [], []
        for g in range(groups):
            cols = slice(g * LANES, (g + 1) * LANES)
            values, keys = stack_heads(v[rows, cols], masks), stack_heads(k[rows, cols], masks)
            out_grad, queries = block_diag(g_att[rows, cols]), block_diag(q[rows, cols])
            soft = probs[p, g].reshape(4, SLOT, PAIR)
            g_probs = dot_nt(values, out_grad).reshape(4, SLOT, PAIR)
            inner = jnp.sum(soft * g_probs, axis=1, keepdims=True)
            g_score = (soft * (g_probs - inner)).reshape(4 * SLOT, PAIR)
            table_sum[g] += g_score
            g_score = g_score.astype(BF16)
            soft = soft.reshape(4 * SLOT, PAIR).astype(BF16)
            g_v = fold(dot(soft, out_grad), masks_f32)
            turned = dot_nt(eye, g_score).astype(BF16)
            g_q = pick(dot(turned, keys)) * scale
            g_k = fold(dot(g_score, queries), masks_f32)
            parts_q.append(jnp.sum(g_q, axis=0, keepdims=True))
            parts_v.append(jnp.sum(g_v, axis=0, keepdims=True))
            g_rows[rows, g * LANES : (g + 1) * LANES] = g_q.astype(BF16)
            g_rows[rows, width + g * LANES : width + (g + 1) * LANES] = g_k.astype(BF16)
            g_rows[rows, 2 * width + g * LANES : 2 * width + (g + 1) * LANES] = g_v.astype(BF16)
        return (
            sum_q + jnp.concatenate(parts_q, axis=1),
            sum_v + jnp.concatenate(parts_v, axis=1),
        )

    sum_q, sum_v = lax.fori_loop(0, n1.shape[0] // PAIR, window_pair, (qv_zero, qv_zero))

    for j in range(3 * groups):
        turned_t[j * LANES : (j + 1) * LANES, :] = dot_nt(
            eye, g_rows[:, j * LANES : (j + 1) * LANES]
        ).astype(BF16)
    g_w[...] = dot(turned_t[...], n1[...]).astype(BF16)

    def deal(far, source, t, slots, start):
        out = q_send if far else q_keep
        for d, s in enumerate(slots):
            for h in range(own_heads):
                for j in range(3):
                    row = pl.multiple_of(j * width + (t * own_heads + h) * HEAD, HEAD)
                    out[s, (h * 3 + j) * HEAD : (h * 3 + j + 1) * HEAD, :] = g_w[
                        pl.ds(row, HEAD), d * lanes : (d + 1) * lanes
                    ]

    each_block(n_dp, tensor, None, None, deal)

    x_hat, inv_std = normalize(dot(place[...], x[...]))
    grad_n1 = dot(g_rows[...], wt[...])
    grad_x = g_mid[...] + norm_back(grad_n1 * vec[0:1, :], x_hat, inv_std)
    g_x[...] = sum(dot(back[...], piece) for piece in split3(grad_x))
    sum_0 = jnp.sum(grad_n1 * x_hat, axis=0, keepdims=True)
    sum_1 = jnp.sum(grad_n1, axis=0, keepdims=True)

    tab[...] = jnp.zeros_like(tab)
    wide = tab.shape[1]
    pulled = []
    for g in range(groups):
        pieces = split3(table_sum[g])
        pulled.append(sum(dot_nt(piece, select[...]) for piece in pieces))
    for g in range(groups):
        table_sum[g] = pulled[g]
    zero = jnp.zeros((4, wide - LANES), F32)
    for a in range(WIN):
        for b in range(WIN):
            shift = ((TABLE - 1) // 2 - SPAN * a - b) % wide
            row = a * CELL + b
            picked = [
                jnp.concatenate([table_sum[g, h * SLOT + row : h * SLOT + row + 1, :] for h in range(4)], axis=0)
                for g in range(groups)
            ]
            both = jnp.concatenate(
                [jnp.concatenate([part, zero], axis=1) for part in picked], axis=0
            )
            tab[...] += pltpu.roll(both, shift, 1)

    me_d, me_t = lax.axis_index("dp"), lax.axis_index("tensor")
    small[...] = jnp.zeros_like(small)
    per_tensor, per_both = width // tensor, width // tensor // n_dp
    for t in range(tensor):
        start = n_dp * (half_slot(t, me_t, tensor) + (tensor // 2) * ((t ^ me_t) & 1))
        for d in range(n_dp):
            s = start + (d ^ me_d)
            cols = slice(d * lanes, (d + 1) * lanes)
            small[s, 0:1, :] = sum_0[:, cols]
            small[s, 1:2, :] = sum_1[:, cols]
            small[s, 2:6, :] = sums[2:6, cols]
            first = (t * per_tensor + d * per_both) // lanes * lanes
            small[s, 6:7, :] = sum_q[:, first : first + lanes]
            small[s, 7:8, :] = sum_v[:, first : first + lanes]
            first = (t * hidden + d * (hidden // n_dp)) // lanes * lanes
            small[s, 8:9, :] = bias_sums[0:1, first : first + lanes]
            for h in range(own_heads):
                for j in range(segments):
                    row = 9 + h * segments + j
                    small[s, row : row + 1, :] = tab[
                        t * own_heads + h : t * own_heads + h + 1, j * lanes : (j + 1) * lanes
                    ]


def make_swaps(n_dp, tensor):
    total = n_dp * tensor

    def swap(value, mask_of):
        return lax.ppermute(value, AXES, [(i, i ^ mask_of(i)) for i in range(total)])

    def first(i):
        return 4 if i & 1 else 2

    def second(i):
        return 2 if i & 1 else 4

    plain = [(lambda i, bit=bit: 1 << bit) for bit in range(tensor.bit_length() - 2, 2, -1)]
    middle = plain + [first, second]
    core = lambda i: 1
    along = [(lambda i, far=far: far * tensor) for far in range(1, n_dp)]
    return swap, along, middle, core


def gather(block, swaps):
    swap, along, middle, core = swaps
    held = jnp.stack([block] + [swap(block, mask) for mask in along])
    for mask in middle:
        held = jnp.concatenate([held, swap(held, mask)], axis=0)
    return held, swap(held, core)


def add(a, b):
    return (a.astype(F32) + b.astype(F32)).astype(a.dtype)


def scatter(send, keep, swaps):
    swap, along, middle, core = swaps
    held = add(keep, swap(send, core))
    for mask in reversed(middle):
        half = held.shape[0] // 2
        held = add(held[:half], swap(held[half:], mask))
    total = held[0].astype(F32)
    for far, mask in enumerate(along):
        total = total + swap(held[far + 1], mask).astype(F32)
    return total


def call(kernel, outs, scratch, args, flops, limit=48 << 20):
    vmem = pl.BlockSpec(memory_space=pltpu.VMEM)
    smem = pl.BlockSpec(memory_space=pltpu.SMEM)
    return pl.pallas_call(
        kernel,
        out_shape=[jax.ShapeDtypeStruct(shape, dtype) for shape, dtype in outs],
        in_specs=[smem if a.dtype == jnp.int32 else vmem for a in args],
        out_specs=[vmem] * len(outs),
        scratch_shapes=[pltpu.VMEM(shape, dtype) for shape, dtype in scratch],
        compiler_params=pltpu.CompilerParams(vmem_limit_bytes=limit),
        cost_estimate=pl.CostEstimate(flops=flops, bytes_accessed=1 << 20, transcendentals=0),
    )(*args)


def per_device(
    block_input,
    out_cotangent,
    live_images,
    width_params,
    w_qkv,
    qv_bias,
    bias_table,
    w_proj,
    fc1_w,
    fc1_bias,
    fc2_w,
):
    n_dp, tensor = lax.axis_size("dp"), lax.axis_size("tensor")
    swaps = make_swaps(n_dp, tensor)
    _, rows_dev, width = block_input.shape
    images = rows_dev // (SIDE * SIDE)
    rows = images * (SIDE // WIN) ** 2 * SLOT
    lanes, columns = w_qkv.shape
    per_tensor = w_proj.shape[0]
    hidden = fc1_w.shape[1]
    heads = width // HEAD
    groups = width // LANES
    half = n_dp * tensor // 2
    place_np, mask_np, select_np = window_constants(images)
    place, back = jnp.asarray(place_np, BF16), jnp.asarray(place_np.T, BF16)
    mask, select = jnp.asarray(mask_np), jnp.asarray(select_np, BF16)
    bind = lambda kernel: functools.partial(kernel, n_dp, tensor)
    x, gy = block_input[0], out_cotangent[0]

    (packed,) = call(
        bind(pack_kernel),
        [((columns + per_tensor + SMALL, lanes), BF16)],
        [((SMALL, LANES), F32)],
        [w_qkv, w_proj, width_params, qv_bias, bias_table, fc1_bias],
        1 << 24,
    )
    own1, other1 = gather(packed, swaps)
    own2, other2 = gather(fc1_w, swaps)
    own3, other3 = gather(fc2_w, swaps)

    wide = 2 * LANES
    n1, q, k, v, wt, vec, probs, att = call(
        bind(forward_kernel),
        [
            ((rows, width), BF16),
            ((rows, width), BF16),
            ((rows, width), BF16),
            ((rows, width), BF16),
            ((3 * width, width), BF16),
            ((16, width), F32),
            ((rows // PAIR, groups, 4 * SLOT, PAIR), F32),
            ((rows, width), BF16),
        ],
        [
            ((width // lanes, 8, lanes), F32),
            ((heads, 8, wide), F32),
            ((heads, wide), F32),
            ((heads, SLOT, LANES), F32),
            ((groups, 4 * SLOT, PAIR), F32),
        ],
        [x, own1, other1, place, select, mask],
        4 << 30,
    )

    outs = [
        ((rows_dev, width), BF16),
        ((rows, width), F32),
        ((rows, width), BF16),
        ((half, lanes, hidden), BF16),
        ((half, lanes, hidden), BF16),
        ((half, lanes, hidden), BF16),
        ((half, lanes, hidden), BF16),
        ((half, per_tensor, lanes), BF16),
        ((half, per_tensor, lanes), BF16),
        ((8, width), F32),
        ((8, hidden * tensor), F32),
    ]
    y, g_mid, g_att, f1_send, f1_keep, f2_send, f2_keep, p_send, p_keep, sums, bias_sums = call(
        bind(middle_kernel),
        outs,
        [
            ((width, width), BF16),
            ((rows, width), BF16),
            ((width, rows), BF16),
            ((rows, width), BF16),
            ((width, rows), BF16),
            ((rows, width), F32),
            ((rows, width), F32),
        ],
        [live_images, x, gy, att, vec, own1, other1, own2, other2, own3, other3, place, back],
        8 << 30,
    )
    g_fc2 = scatter(f2_send, f2_keep, swaps)
    g_fc1 = scatter(f1_send, f1_keep, swaps)
    g_proj = scatter(p_send, p_keep, swaps)

    g_x, q_send, q_keep, small = call(
        bind(backward_kernel),
        [
            ((rows_dev, width), F32),
            ((half, columns, lanes), BF16),
            ((half, columns, lanes), BF16),
            ((2 * half, 16, lanes), F32),
        ],
        [
            ((rows, 3 * width), BF16),
            ((groups, 4 * SLOT, PAIR), F32),
            ((3 * width, width), BF16),
            ((heads, wide), F32),
            ((3 * width, rows), BF16),
        ],
        [x, n1, q, k, v, probs, wt, vec, g_att, g_mid, sums, bias_sums, place, back, select],
        6 << 30,
    )
    g_qkv = scatter(q_send, q_keep, swaps)
    small = scatter(small[half:], small[:half], swaps)

    me = lax.axis_index("tensor") * n_dp + lax.axis_index("dp")
    count = qv_bias.shape[2]
    g_qv = lax.dynamic_slice(small[6:8], (0, lax.rem(me * count, lanes)), (2, count))
    count = fc1_bias.shape[1]
    g_b1 = lax.dynamic_slice(small[8:9], (0, lax.rem(me * count, lanes)), (1, count))
    own_heads = bias_table.shape[0]
    g_table = small[9 : 9 + own_heads * pl.cdiv(TABLE, lanes)].reshape(own_heads, -1)[:, :TABLE]
    return (
        y[None],
        g_x[None],
        small[0:6],
        g_qkv.T,
        g_qv[:, None, :],
        g_table,
        g_proj,
        g_fc1,
        g_b1,
        g_fc2.T,
    )


def solution(mesh):
    rows = P(None, AXES, None)
    placed = (
        rows,
        rows,
        P("dp"),
        P(None, "dp"),
        P("dp", "tensor"),
        P(None, "tensor", "dp"),
        P("tensor", None),
        P("tensor", "dp"),
        P("dp", "tensor"),
        P("tensor", "dp"),
        P("tensor", "dp"),
    )
    return jax.shard_map(
        per_device,
        mesh=mesh,
        in_specs=placed,
        out_specs=(rows, rows) + placed[3:],
        check_vma=False,
    )
```

time: 668 us -> 185 us (0.28)
  waiting for transfers between devices: 323 us -> 59.2 us
  blocking collectives: 123 us -> 0 us
  local copies, waits for them, and re-layouts: 117 us -> 12.5 us
  starting transfers between devices: 1.09 us -> 62.7 us
  matrix products: 53.8 us -> 0 us
  Pallas kernels: 0 us -> 39.7 us
  other arithmetic: 29.3 us -> 8.23 us
  between operations: 16.3 us -> 1.97 us
    reduce_scatter x5 -> x0, waiting for transfers between devices: 217 us -> none  [the longest x1 61 us: per_device(): lax.psum_scatter(jnp.dot(heads_out, w_out, preferred_element_type=jnp.flo...]
    all_gather x6 -> x0, blocking collectives: 79.2 us -> none  [the longest x1 13.8 us: per_device(): w_first = lax.all_gather(fc1_w, 'dp', axis=0, tiled=True)]
    unnamed x21 -> x0, waiting for transfers between devices: 63.1 us -> none
    ppermute x0 -> x48, starting transfers between devices: none -> 62.7 us  [swap(): lax.ppermute(value, AXES, [(i, i ^ mask_of(i)) for i in range(total)])]
    ppermute x0 -> x48, waiting for transfers between devices: none -> 59.2 us  [swap(): lax.ppermute(value, AXES, [(i, i ^ mask_of(i)) for i in range(total)])]
    dot_general x20 -> x0, matrix products: 53.8 us -> none  [the longest x4 13.8 us: times_transposed(): lax.dot_general(left, right, (((1,), (1,)), ((), ())), preferred_element_...]
    all_gather x4 -> x0, waiting for transfers between devices: 43.6 us -> none  [the longest x1 23.2 us: per_device(): grad_mid_all = lax.all_gather(grad_mid_b, 'tensor', axis=0, tiled=True)]
    pallas_call x0 -> x4, Pallas kernels: none -> 39.7 us  [call(): pl.pallas_call(kernel, out_shape=[jax.ShapeDtypeStruct(shape, dtype) for...]
  transfers between devices with their start and end apart: 15 -> 48, of which waited for: 11 -> 21; matrix products, arithmetic and copies ran while one was open for 14% -> 7% of each run, Pallas kernels for 0% -> 4%
where the time goes in v1:
time: 185 us; the launch traced here: 184 us
  starting transfers between devices  62.7 us (34%)
  waiting for transfers between devices  59.2 us (32%)
  Pallas kernels  39.7 us (21%)
  local copies, waits for them, and re-layouts  12.5 us (7%)
  other arithmetic  8.23 us (4%)
  between operations  1.97 us (1%)
    ppermute x48, starting transfers between devices, swap(): lax.ppermute(value, AXES, [(i, i ^ mask_of(i)) for i in range(total)])  62.7 us
    ppermute x48, waiting for transfers between devices, swap(): lax.ppermute(value, AXES, [(i, i ^ mask_of(i)) for i in range(total)])  59.2 us
    pallas_call x4, Pallas kernels, call(): pl.pallas_call(kernel, out_shape=[jax.ShapeDtypeStruct(shape, dtype) for...  39.7 us
    unnamed x55, local copies, waits for them, and re-layouts  9.4 us
    convert_element_type x12, other arithmetic, add(): return (a.astype(F32) + b.astype(F32)).astype(a.dtype)  5.23 us
  transfers between devices with their start and end apart: 48, of which 21 were waited for; matrix products, arithmetic and copies ran while one was open for 7% of the time, Pallas kernels for 4%

profile of v1, /device:TPU:0, one launch (start us, length us, event | category | flops | bytes accessed | tf_op | source)
XLA Modules:
  0.0 184.3 jit_solution(16960444415661763561)
XLA Ops:
  0.7 0.9 copy.25.wq
  2.3 0.7 copy-done
  3.0 0.7 copy-done.2
  3.7 0.7 copy-done.3
  5.2 3.1 %collective-permute-start = (bf16[288,128]{1,0:T(8,128)(2,1)S(1)}, bf16[288,128]{1,0:T(8,128)(2,1)S(1)}, u32[]{:S(2)}, u32[]{:S(2)}) collective-permute-start(bf16[288,128]{1,0:T(8,128)(2,1)S(1)} %shard_map.222), channel_id=1, source_target_pairs={{0,8},{1,9},{2,10},{3,11},{4,12},{5,13},{6,14},{7,15},{8,0},{9,1},... | collective-permute-start | bytes 221192 | tf_op jit(solution)/shard_map/ppermute | solution.py:466
  8.3 2.6 %collective-permute-start.1 = (bf16[288,128]{1,0:T(8,128)(2,1)S(1)}, bf16[288,128]{1,0:T(8,128)(2,1)S(1)}, u32[]{:S(2)}, u32[]{:S(2)}) collective-permute-start(bf16[288,128]{1,0:T(8,128)(2,1)S(1)} %shard_map.222), channel_id=1, source_target_pairs={{0,16},{1,17},{2,18},{3,19},{4,20},{5,21},{6,22},{7,23},{8,24},{9,... | collective-permute-start | bytes 221192 | tf_op jit(solution)/shard_map/ppermute | solution.py:466
  11.3 3.9 %collective-permute-start.14 = (bf16[256,128]{1,0:T(8,128)(2,1)}, bf16[256,128]{1,0:T(8,128)(2,1)S(1)}, u32[]{:S(2)}, u32[]{:S(2)}) collective-permute-start(bf16[256,128]{1,0:T(8,128)(2,1)} %param.25), channel_id=1, source_target_pairs={{0,24},{1,25},{2,26},{3,27},{4,28},{5,29},{6,30},{7,31},{8,16},{9,... | collective-permute-start | bytes 196616 | tf_op jit(solution)/shard_map/ppermute | solution.py:466
  15.3 0.9 constant_dynamic-update-slice_fusion.26
  16.1 0.9 constant_dynamic-update-slice_fusion.15
  17.1 2.6 %collective-permute-done.13 = bf16[256,128]{1,0:T(8,128)(2,1)S(1)} collective-permute-done((bf16[256,128]{1,0:T(8,128)(2,1)}, bf16[256,128]{1,0:T(8,128)(2,1)S(1)}, u32[]{:S(2)}, u32[]{:S(2)}) %collective-permute-start.13) | collective-permute-done | bytes 65568 | tf_op jit(solution)/shard_map/ppermute | solution.py:466
  19.7 3.2 %collective-permute-start.8 = (bf16[128,256]{1,0:T(8,128)(2,1)}, bf16[128,256]{1,0:T(8,128)(2,1)S(1)}, u32[]{:S(2)}, u32[]{:S(2)}) collective-permute-start(bf16[128,256]{1,0:T(8,128)(2,1)} %param.23), channel_id=1, source_target_pairs={{0,24},{1,25},{2,26},{3,27},{4,28},{5,29},{6,30},{7,31},{8,16},{9,... | collective-permute-start | bytes 196616 | tf_op jit(solution)/shard_map/ppermute | solution.py:466
  22.9 0.9 pad_maximum_fusion.2
  23.8 0.7 collective-permute-start.2
  24.5 3.2 %collective-permute-done.7 = bf16[128,256]{1,0:T(8,128)(2,1)S(1)} collective-permute-done((bf16[128,256]{1,0:T(8,128)(2,1)}, bf16[128,256]{1,0:T(8,128)(2,1)S(1)}, u32[]{:S(2)}, u32[]{:S(2)}) %collective-permute-start.7) | collective-permute-done | bytes 65568 | tf_op jit(solution)/shard_map/ppermute | solution.py:466
  27.7 1.5 collective-permute-start.15
  30.1 1.6 collective-permute-start.3
  31.8 12.7 %collective-permute-done.3 = bf16[4,288,128]{2,1,0:T(8,128)(2,1)S(1)} collective-permute-done((bf16[4,288,128]{2,1,0:T(8,128)(2,1)S(1)}, bf16[4,288,128]{2,1,0:T(8,128)(2,1)S(1)}, u32[]{:S(2)}, u32[]{:S(2)}) %collective-permute-start.3) | collective-permute-done | bytes 294944 | tf_op jit(solution)/shard_map/ppermute | solution.py:466
  44.6 1.6 collective-permute-start.4
  46.9 1.6 collective-permute-start.10
  48.5 6.0 %collective-permute-done.4 = bf16[8,288,128]{2,1,0:T(8,128)(2,1)S(1)} collective-permute-done((bf16[8,288,128]{2,1,0:T(8,128)(2,1)S(1)}, bf16[8,288,128]{2,1,0:T(8,128)(2,1)S(1)}, u32[]{:S(2)}, u32[]{:S(2)}) %collective-permute-start.4) | collective-permute-done | bytes 589856 | tf_op jit(solution)/shard_map/ppermute | solution.py:466
  54.7 5.4 %collective-permute-done.16 = bf16[8,256,128]{2,1,0:T(8,128)(2,1)S(1)} collective-permute-done((bf16[8,256,128]{2,1,0:T(8,128)(2,1)S(1)}, bf16[8,256,128]{2,1,0:T(8,128)(2,1)S(1)}, u32[]{:S(2)}, u32[]{:S(2)}) %collective-permute-start.16) | collective-permute-done | bytes 524320 | tf_op jit(solution)/shard_map/ppermute | solution.py:466
  60.3 5.5 %collective-permute-done.10 = bf16[8,128,256]{2,1,0:T(8,128)(2,1)S(1)} collective-permute-done((bf16[8,128,256]{2,1,0:T(8,128)(2,1)S(1)}, bf16[8,128,256]{2,1,0:T(8,128)(2,1)S(1)}, u32[]{:S(2)}, u32[]{:S(2)}) %collective-permute-start.10) | collective-permute-done | bytes 524320 | tf_op jit(solution)/shard_map/ppermute | solution.py:466
  66.6 7.3 %shard_map.223 = (bf16[512,512]{1,0:T(8,128)(2,1)S(1)}, bf16[512,512]{1,0:T(8,128)(2,1)S(1)}, bf16[512,512]{1,0:T(8,128)(2,1)S(1)}, bf16[512,512]{1,0:T(8,128)(2...) custom-call(bf16[392,512]{1,0:T(8,128)(2,1)S(1)} %bitcast.108, ...), custom_call_target="tpu_custom_call" | custom-call | flops 4294967296 | bytes 1048576 | tf_op jit(solution)/shard_map/pallas_call | solution.py:508
  74.0 0.9 copy-done.18
  75.4 17.6 %shard_map.224 = (bf16[392,512]{1,0:T(8,128)(2,1)}, f32[512,512]{1,0:T(8,128)S(1)}, bf16[512,512]{1,0:T(8,128)(2,1)S(1)}, bf16[16,128,256]{2,1,0:T(8,128)(2,1)S(...) custom-call(s32[1]{0:T(128)S(6)} %copy.56.live, ...), custom_call_target="tpu_custom_call" | custom-call | flops 8589934592 | bytes 1048576 | tf_op jit(solution)/shard_map/pallas_call | solution.py:508
  92.9 1.0 copy-done.12
  93.9 14.7 %shard_map.225 = (f32[392,512]{1,0:T(8,128)}, bf16[16,192,128]{2,1,0:T(8,128)(2,1)S(1)}, bf16[16,192,128]{2,1,0:T(8,128)(2,1)S(1)}, f32[32,16,128]{2,1,0:T(8,128)S(1)}) custom-call(bf16[392,512]{1,0:T(8,128)(2,1)S(1)} %bitcast.110, bf16[512,512]{1,0:T(8,128)(2,1)S(1)} %get-tuple-element.36.n1, bf16[512,512]{1,0:T(8,128)(2,1)S(1)} %get-tuple-element.37.q, ...), custom_call_target="tpu_custom_call" | custom-call | flops 6442450944 | bytes 1048576 | tf_op jit(solution)/shard_map/pallas_call | solution.py:508
  109.2 1.0 collective-permute-done.18
  110.2 1.6 collective-permute-start.19
  111.8 2.7 %collective-permute-done.19 = f32[8,16,128]{2,1,0:T(8,128)S(1)} collective-permute-done((f32[8,16,128]{2,1,0:T(8,128)S(1)}, f32[8,16,128]{2,1,0:T(8,128)S(1)}, u32[]{:S(2)}, u32[]{:S(2)}) %collective-permute-start.19) | collective-permute-done | bytes 65568 | tf_op jit(solution)/shard_map/ppermute | solution.py:466
  114.5 1.6 collective-permute-start.20
  116.6 1.9 %collective-permute-done.20 = f32[4,16,128]{2,1,0:T(8,128)S(1)} collective-permute-done((f32[4,16,128]{2,1,0:T(8,128)S(1)}, f32[4,16,128]{2,1,0:T(8,128)S(1)}, u32[]{:S(2)}, u32[]{:S(2)}) %collective-permute-start.20) | collective-permute-done | bytes 32800 | tf_op jit(solution)/shard_map/ppermute | solution.py:466
  118.6 1.7 collective-permute-start.22
  120.8 2.1 %collective-permute-start.23 = (f32[16,128]{1,0:T(8,128)S(1)}, f32[16,128]{1,0:T(8,128)S(1)}, u32[]{:S(2)}, u32[]{:S(2)}) collective-permute-start(f32[16,128]{1,0:T(8,128)S(1)} %get-tuple-element.109), channel_id=1, source_target_pairs={{0,24},{1,25},{2,26},{3,27},{4,28},{5,29},{6,30},{7,31},{8,16},{9,... | collective-permute-start | bytes 24584 | tf_op jit(solution)/shard_map/ppermute | solution.py:466
  123.2 1.6 collective-permute-start.31
  124.8 1.5 collective-permute-done.23
  128.3 1.6 collective-permute-start.32
  130.4 2.2 %collective-permute-done.32 = bf16[4,64,128]{2,1,0:T(8,128)(2,1)S(1)} collective-permute-done((bf16[4,64,128]{2,1,0:T(8,128)(2,1)S(1)}, bf16[4,64,128]{2,1,0:T(8,128)(2,1)S(1)}, u32[]{:S(2)}, u32[]{:S(2)}) %collective-permute-start.32) | collective-permute-done | bytes 65568 | tf_op jit(solution)/shard_map/ppermute | solution.py:466
  132.6 1.4 add_convert_fusion.2
  134.1 1.6 collective-permute-start.25
  135.7 2.8 %collective-permute-start.33 = (bf16[64,128]{1,0:T(8,128)(2,1)S(1)}, bf16[64,128]{1,0:T(8,128)(2,1)S(1)}, u32[]{:S(2)}, u32[]{:S(2)}) collective-permute-start(bf16[64,128]{1,0:T(8,128)(2,1)S(1)} %get-tuple-element.89), channel_id=1, source_target_pairs={{0,8},{1,9},{2,10},{3,11},{4,12},{5,13},{6,14},{7,15},{8,0},{9,1},... | collective-permute-start | bytes 49160 | tf_op jit(solution)/shard_map/ppermute | solution.py:466
  138.5 2.4 %collective-permute-start.35 = (bf16[64,128]{1,0:T(8,128)(2,1)S(1)}, bf16[64,128]{1,0:T(8,128)(2,1)S(1)}, u32[]{:S(2)}, u32[]{:S(2)}) collective-permute-start(bf16[64,128]{1,0:T(8,128)(2,1)S(1)} %get-tuple-element.90), channel_id=1, source_target_pairs={{0,24},{1,25},{2,26},{3,27},{4,28},{5,29},{6,30},{7,31},{8,16},{9,... | collective-permute-start | bytes 49160 | tf_op jit(solution)/shard_map/ppermute | solution.py:466
  140.9 1.5 add_convert_fusion
  142.5 1.0 collective-permute-start.43
  143.6 1.6 collective-permute-start.26
  145.2 1.5 add_convert_fusion.1
  146.8 4.7 %collective-permute-done.26 = bf16[4,192,128]{2,1,0:T(8,128)(2,1)S(1)} collective-permute-done((bf16[4,192,128]{2,1,0:T(8,128)(2,1)S(1)}, bf16[4,192,128]{2,1,0:T(8,128)(2,1)S(1)}, u32[]{:S(2)}, u32[]{:S(2)}) %collective-permute-start.26) | collective-permute-done | bytes 196640 | tf_op jit(solution)/shard_map/ppermute | solution.py:466
  151.5 1.1 collective-permute-start.37
  152.7 3.9 %collective-permute-start.27 = (bf16[192,128]{1,0:T(8,128)(2,1)S(1)}, bf16[192,128]{1,0:T(8,128)(2,1)S(1)}, u32[]{:S(2)}, u32[]{:S(2)}) collective-permute-start(bf16[192,128]{1,0:T(8,128)(2,1)S(1)} %get-tuple-element.78), channel_id=1, source_target_pairs={{0,8},{1,9},{2,10},{3,11},{4,12},{5,13},{6,14},{7,15},{8,0},{9,1},... | collective-permute-start | bytes 147464 | tf_op jit(solution)/shard_map/ppermute | solution.py:466
  156.6 2.4 %collective-permute-start.29 = (bf16[192,128]{1,0:T(8,128)(2,1)S(1)}, bf16[192,128]{1,0:T(8,128)(2,1)S(1)}, u32[]{:S(2)}, u32[]{:S(2)}) collective-permute-start(bf16[192,128]{1,0:T(8,128)(2,1)S(1)} %get-tuple-element.79), channel_id=1, source_target_pairs={{0,24},{1,25},{2,26},{3,27},{4,28},{5,29},{6,30},{7,31},{8,16},{9,... | collective-permute-start | bytes 147464 | tf_op jit(solution)/shard_map/ppermute | solution.py:466
  159.7 2.0 %collective-permute-done.28 = bf16[192,128]{1,0:T(8,128)(2,1)S(1)} collective-permute-done((bf16[192,128]{1,0:T(8,128)(2,1)S(1)}, bf16[192,128]{1,0:T(8,128)(2,1)S(1)}, u32[]{:S(2)}, u32[]{:S(2)}) %collective-permute-start.28) | collective-permute-done | bytes 49184 | tf_op jit(solution)/shard_map/ppermute | solution.py:466
  161.6 1.0 collective-permute-done.29
  162.7 0.7 fusion.7
  163.5 2.1 %collective-permute-start.44 = (bf16[4,128,256]{2,1,0:T(8,128)(2,1)S(1)}, bf16[4,128,256]{2,1,0:T(8,128)(2,1)S(1)}, u32[]{:S(2)}, u32[]{:S(2)}) collective-permute-start(bf16[4,128,256]{2,1,0:T(8,128)(2,1)S(1)} %slice.228), channel_id=1, source_target_pairs={{0,2},{1,5},{2,0},{3,7},{4,6},{5,1},{6,4},{7,3},{8,10},{9,13},{10,... | collective-permute-start | bytes 786440 | tf_op jit(solution)/shard_map/ppermute | solution.py:466
  165.8 2.0 %collective-permute-start.38 = (bf16[4,128,256]{2,1,0:T(8,128)(2,1)S(1)}, bf16[4,128,256]{2,1,0:T(8,128)(2,1)S(1)}, u32[]{:S(2)}, u32[]{:S(2)}) collective-permute-start(bf16[4,128,256]{2,1,0:T(8,128)(2,1)S(1)} %slice.219), channel_id=1, source_target_pairs={{0,2},{1,5},{2,0},{3,7},{4,6},{5,1},{6,4},{7,3},{8,10},{9,13},{10,... | collective-permute-start | bytes 786440 | tf_op jit(solution)/shard_map/ppermute | solution.py:466
  167.7 2.2 %collective-permute-done.44 = bf16[4,128,256]{2,1,0:T(8,128)(2,1)S(1)} collective-permute-done((bf16[4,128,256]{2,1,0:T(8,128)(2,1)S(1)}, bf16[4,128,256]{2,1,0:T(8,128)(2,1)S(1)}, u32[]{:S(2)}, u32[]{:S(2)}) %collective-permute-start.44) | collective-permute-done | bytes 262176 | tf_op jit(solution)/shard_map/ppermute | solution.py:466
  170.7 2.3 %collective-permute-start.46 = (bf16[128,256]{1,0:T(8,128)(2,1)S(1)}, bf16[128,256]{1,0:T(8,128)(2,1)S(1)}, u32[]{:S(2)}, u32[]{:S(2)}) collective-permute-start(bf16[128,256]{1,0:T(8,128)(2,1)S(1)} %get-tuple-element.70), channel_id=1, source_target_pairs={{0,16},{1,17},{2,18},{3,19},{4,20},{5,21},{6,22},{7,23},{8,24},{9,... | collective-permute-start | bytes 196616 | tf_op jit(solution)/shard_map/ppermute | solution.py:466
  173.0 1.4 collective-permute-start.47
  174.6 0.7 collective-permute-start.39
  175.3 2.3 %collective-permute-start.40 = (bf16[128,256]{1,0:T(8,128)(2,1)S(1)}, bf16[128,256]{1,0:T(8,128)(2,1)S(1)}, u32[]{:S(2)}, u32[]{:S(2)}) collective-permute-start(bf16[128,256]{1,0:T(8,128)(2,1)S(1)} %get-tuple-element.73), channel_id=1, source_target_pairs={{0,16},{1,17},{2,18},{3,19},{4,20},{5,21},{6,22},{7,23},{8,24},{9,... | collective-permute-start | bytes 196616 | tf_op jit(solution)/shard_map/ppermute | solution.py:466
  177.6 1.4 collective-permute-start.41
  179.2 0.8 copy.28
  180.5 3.2 %collective-permute-done.41 = bf16[128,256]{1,0:T(8,128)(2,1)S(1)} collective-permute-done((bf16[128,256]{1,0:T(8,128)(2,1)S(1)}, bf16[128,256]{1,0:T(8,128)(2,1)S(1)}, u32[]{:S(2)}, u32[]{:S(2)}) %collective-permute-start.41) | collective-permute-done | bytes 65568 | tf_op jit(solution)/shard_map/ppermute | solution.py:466
  183.7 0.7 fusion.4
  (143 shorter events, 12.0 us)
Async XLA Ops:
  0.6 28.5 %copy-start.15 = (bf16[128,256]{1,0:T(8,128)(2,1)S(1)}, bf16[128,256]{1,0:T(8,128)(2,1)}, u32[]{:S(2)}) copy-start(bf16[128,256]{1,0:T(8,128)(2,1)} %param.23) | copy-start | bytes 196612
  5.2 24.7 %collective-permute-start = (bf16[288,128]{1,0:T(8,128)(2,1)S(1)}, bf16[288,128]{1,0:T(8,128)(2,1)S(1)}, u32[]{:S(2)}, u32[]{:S(2)}) collective-permute-start(bf16[288,128]{1,0:T(8,128)(2,1)S(1)} %shard_map.222), channel_id=1, source_target_pairs={{0,8},{1,9},{2,10},{3,11},{4,12},{5,13},{6,14},{7,15},{8,0},{9,1},... | collective-permute-start | bytes 221192 | tf_op jit(solution)/shard_map/ppermute | solution.py:466
  8.3 21.6 %collective-permute-start.1 = (bf16[288,128]{1,0:T(8,128)(2,1)S(1)}, bf16[288,128]{1,0:T(8,128)(2,1)S(1)}, u32[]{:S(2)}, u32[]{:S(2)}) collective-permute-start(bf16[288,128]{1,0:T(8,128)(2,1)S(1)} %shard_map.222), channel_id=1, source_target_pairs={{0,16},{1,17},{2,18},{3,19},{4,20},{5,21},{6,22},{7,23},{8,24},{9,... | collective-permute-start | bytes 221192 | tf_op jit(solution)/shard_map/ppermute | solution.py:466
  10.9 6.1 %collective-permute-start.12 = (bf16[256,128]{1,0:T(8,128)(2,1)}, bf16[256,128]{1,0:T(8,128)(2,1)S(1)}, u32[]{:S(2)}, u32[]{:S(2)}) collective-permute-start(bf16[256,128]{1,0:T(8,128)(2,1)} %param.25), channel_id=1, source_target_pairs={{0,8},{1,9},{2,10},{3,11},{4,12},{5,13},{6,14},{7,15},{8,0},{9,1},... | collective-permute-start | bytes 196616 | tf_op jit(solution)/shard_map/ppermute | solution.py:466
  11.3 8.4 %collective-permute-start.13 = (bf16[256,128]{1,0:T(8,128)(2,1)}, bf16[256,128]{1,0:T(8,128)(2,1)S(1)}, u32[]{:S(2)}, u32[]{:S(2)}) collective-permute-start(bf16[256,128]{1,0:T(8,128)(2,1)} %param.25), channel_id=1, source_target_pairs={{0,16},{1,17},{2,18},{3,19},{4,20},{5,21},{6,22},{7,23},{8,24},{9,... | collective-permute-start | bytes 196616 | tf_op jit(solution)/shard_map/ppermute | solution.py:466
  11.3 8.4 %collective-permute-start.14 = (bf16[256,128]{1,0:T(8,128)(2,1)}, bf16[256,128]{1,0:T(8,128)(2,1)S(1)}, u32[]{:S(2)}, u32[]{:S(2)}) collective-permute-start(bf16[256,128]{1,0:T(8,128)(2,1)} %param.25), channel_id=1, source_target_pairs={{0,24},{1,25},{2,26},{3,27},{4,28},{5,29},{6,30},{7,31},{8,16},{9,... | collective-permute-start | bytes 196616 | tf_op jit(solution)/shard_map/ppermute | solution.py:466
  17.0 6.8 %collective-permute-start.6 = (bf16[128,256]{1,0:T(8,128)(2,1)}, bf16[128,256]{1,0:T(8,128)(2,1)S(1)}, u32[]{:S(2)}, u32[]{:S(2)}) collective-permute-start(bf16[128,256]{1,0:T(8,128)(2,1)} %param.23), channel_id=1, source_target_pairs={{0,8},{1,9},{2,10},{3,11},{4,12},{5,13},{6,14},{7,15},{8,0},{9,1},... | collective-permute-start | bytes 196616 | tf_op jit(solution)/shard_map/ppermute | solution.py:466
  19.7 7.9 %collective-permute-start.7 = (bf16[128,256]{1,0:T(8,128)(2,1)}, bf16[128,256]{1,0:T(8,128)(2,1)S(1)}, u32[]{:S(2)}, u32[]{:S(2)}) collective-permute-start(bf16[128,256]{1,0:T(8,128)(2,1)} %param.23), channel_id=1, source_target_pairs={{0,16},{1,17},{2,18},{3,19},{4,20},{5,21},{6,22},{7,23},{8,24},{9,... | collective-permute-start | bytes 196616 | tf_op jit(solution)/shard_map/ppermute | solution.py:466
  19.7 9.4 %collective-permute-start.8 = (bf16[128,256]{1,0:T(8,128)(2,1)}, bf16[128,256]{1,0:T(8,128)(2,1)S(1)}, u32[]{:S(2)}, u32[]{:S(2)}) collective-permute-start(bf16[128,256]{1,0:T(8,128)(2,1)} %param.23), channel_id=1, source_target_pairs={{0,24},{1,25},{2,26},{3,27},{4,28},{5,29},{6,30},{7,31},{8,16},{9,... | collective-permute-start | bytes 196616 | tf_op jit(solution)/shard_map/ppermute | solution.py:466
  23.8 6.3 %collective-permute-start.2 = (bf16[288,128]{1,0:T(8,128)(2,1)S(1)}, bf16[288,128]{1,0:T(8,128)(2,1)S(1)}, u32[]{:S(2)}, u32[]{:S(2)}) collective-permute-start(bf16[288,128]{1,0:T(8,128)(2,1)S(1)} %shard_map.222), channel_id=1, source_target_pairs={{0,24},{1,25},{2,26},{3,27},{4,28},{5,29},{6,30},{7,31},{8,16},{9,... | collective-permute-start | bytes 221192 | tf_op jit(solution)/shard_map/ppermute | solution.py:466
  27.7 18.5 %collective-permute-start.15 = (bf16[4,256,128]{2,1,0:T(8,128)(2,1)S(1)}, bf16[4,256,128]{2,1,0:T(8,128)(2,1)S(1)}, u32[]{:S(2)}, u32[]{:S(2)}) collective-permute-start(bf16[4,256,128]{2,1,0:T(8,128)(2,1)S(1)} %pad_maximum_fusion.2), channel_id=1, source_target_pairs={{0,2},{1,5},{2,0},{3,7},{4,6},{5,1},{6,4},{7,3},{8,10},{9,13},{10,... | collective-permute-start | bytes 786440 | tf_op jit(solution)/shard_map/ppermute | solution.py:466
  29.2 17.7 %collective-permute-start.9 = (bf16[4,128,256]{2,1,0:T(8,128)(2,1)S(1)}, bf16[4,128,256]{2,1,0:T(8,128)(2,1)S(1)}, u32[]{:S(2)}, u32[]{:S(2)}) collective-permute-start(bf16[4,128,256]{2,1,0:T(8,128)(2,1)S(1)} %pad_maximum_fusion.1), channel_id=1, source_target_pairs={{0,2},{1,5},{2,0},{3,7},{4,6},{5,1},{6,4},{7,3},{8,10},{9,13},{10,... | collective-permute-start | bytes 786440 | tf_op jit(solution)/shard_map/ppermute | solution.py:466
  30.1 14.3 %collective-permute-start.3 = (bf16[4,288,128]{2,1,0:T(8,128)(2,1)S(1)}, bf16[4,288,128]{2,1,0:T(8,128)(2,1)S(1)}, u32[]{:S(2)}, u32[]{:S(2)}) collective-permute-start(bf16[4,288,128]{2,1,0:T(8,128)(2,1)S(1)} %pad_maximum_fusion), channel_id=1, source_target_pairs={{0,2},{1,5},{2,0},{3,7},{4,6},{5,1},{6,4},{7,3},{8,10},{9,13},{10,... | collective-permute-start | bytes 884744 | tf_op jit(solution)/shard_map/ppermute | solution.py:466
  44.6 9.9 %collective-permute-start.4 = (bf16[8,288,128]{2,1,0:T(8,128)(2,1)S(1)}, bf16[8,288,128]{2,1,0:T(8,128)(2,1)S(1)}, u32[]{:S(2)}, u32[]{:S(2)}) collective-permute-start(bf16[8,288,128]{2,1,0:T(8,128)(2,1)S(1)} %get-tuple-element.66), channel_id=1, source_target_pairs={{0,4},{1,3},{2,6},{3,1},{4,0},{5,7},{6,2},{7,5},{8,12},{9,11},{10,... | collective-permute-start | bytes 1769480 | tf_op jit(solution)/shard_map/ppermute | solution.py:466
  46.3 13.8 %collective-permute-start.16 = (bf16[8,256,128]{2,1,0:T(8,128)(2,1)S(1)}, bf16[8,256,128]{2,1,0:T(8,128)(2,1)S(1)}, u32[]{:S(2)}, u32[]{:S(2)}) collective-permute-start(bf16[8,256,128]{2,1,0:T(8,128)(2,1)S(1)} %get-tuple-element.74), channel_id=1, source_target_pairs={{0,4},{1,3},{2,6},{3,1},{4,0},{5,7},{6,2},{7,5},{8,12},{9,11},{10,... | collective-permute-start | bytes 1572872 | tf_op jit(solution)/shard_map/ppermute | solution.py:466
  46.9 18.8 %collective-permute-start.10 = (bf16[8,128,256]{2,1,0:T(8,128)(2,1)S(1)}, bf16[8,128,256]{2,1,0:T(8,128)(2,1)S(1)}, u32[]{:S(2)}, u32[]{:S(2)}) collective-permute-start(bf16[8,128,256]{2,1,0:T(8,128)(2,1)S(1)} %get-tuple-element.76), channel_id=1, source_target_pairs={{0,4},{1,3},{2,6},{3,1},{4,0},{5,7},{6,2},{7,5},{8,12},{9,11},{10,... | collective-permute-start | bytes 1572872 | tf_op jit(solution)/shard_map/ppermute | solution.py:466
  54.6 19.4 %copy-start.1 = (bf16[16,288,128]{2,1,0:T(8,128)(2,1)}, bf16[16,288,128]{2,1,0:T(8,128)(2,1)S(1)}, u32[]{:S(2)}) copy-start(bf16[16,288,128]{2,1,0:T(8,128)(2,1)S(1)} %constant_dynamic-update-slice_fusion.5.own.own1) | copy-start | bytes 3538948
  54.6 12.0 %copy-start.7 = (bf16[1,392,512]{2,1,0:T(8,128)(2,1)S(1)}, bf16[1,392,512]{2,1,0:T(8,128)(2,1)}, u32[]{:S(2)}) copy-start(bf16[1,392,512]{2,1,0:T(8,128)(2,1)} %param.15) | copy-start | bytes 1204228
  54.6 12.0 %copy-start.8 = (bf16[512,392]{1,0:T(8,128)(2,1)S(1)}, bf16[512,392]{1,0:T(8,128)(2,1)}, u32[]{:S(2)}) copy-start(bf16[512,392]{1,0:T(8,128)(2,1)} %constant.31.clone.place) | copy-start | bytes 1204228
  54.6 12.0 %copy-start.10 = (f32[2,64,128]{2,1,0:T(8,128)S(1)}, f32[2,64,128]{2,1,0:T(8,128)}, u32[]{:S(2)}) copy-start(f32[2,64,128]{2,1,0:T(8,128)} %constant.33.clone.mask) | copy-start | bytes 196612
  54.6 12.0 %copy-start.11 = (bf16[128,128]{1,0:T(8,128)(2,1)S(1)}, bf16[128,128]{1,0:T(8,128)(2,1)}, u32[]{:S(2)}) copy-start(bf16[128,128]{1,0:T(8,128)(2,1)} %constant.34.clone.select) | copy-start | bytes 98308
  54.7 11.9 %collective-permute-start.5 = (bf16[16,288,128]{2,1,0:T(8,128)(2,1)S(1)}, bf16[16,288,128]{2,1,0:T(8,128)(2,1)S(1)}, u32[]{:S(2)}, u32[]{:S(2)}) collective-permute-start(bf16[16,288,128]{2,1,0:T(8,128)(2,1)S(1)} %constant_dynamic-update-slice_fusion.5.own.own1), channel_id=1, source_target_pairs={{0,1},{1,0},{2,3},{3,2},{4,5},{5,4},{6,7},{7,6},{8,9},{9,8},{10,11... | collective-permute-start | bytes 3538952 | tf_op jit(solution)/shard_map/ppermute | solution.py:466
  60.2 13.8 %copy-start.17 = (bf16[16,256,128]{2,1,0:T(8,128)(2,1)}, bf16[16,256,128]{2,1,0:T(8,128)(2,1)S(1)}, u32[]{:S(2)}) copy-start(bf16[16,256,128]{2,1,0:T(8,128)(2,1)S(1)} %constant_dynamic-update-slice_fusion.27.own3) | copy-start | bytes 3145732
  60.2 13.8 %collective-permute-start.17 = (bf16[16,256,128]{2,1,0:T(8,128)(2,1)S(1)}, bf16[16,256,128]{2,1,0:T(8,128)(2,1)S(1)}, u32[]{:S(2)}, u32[]{:S(2)}) collective-permute-start(bf16[16,256,128]{2,1,0:T(8,128)(2,1)S(1)} %constant_dynamic-update-slice_fusion.27.own3), channel_id=1, source_target_pairs={{0,1},{1,0},{2,3},{3,2},{4,5},{5,4},{6,7},{7,6},{8,9},{9,8},{10,11... | collective-permute-start | bytes 3145736 | tf_op jit(solution)/shard_map/ppermute | solution.py:466
  65.8 8.2 %copy-start.16 = (bf16[16,128,256]{2,1,0:T(8,128)(2,1)}, bf16[16,128,256]{2,1,0:T(8,128)(2,1)S(1)}, u32[]{:S(2)}) copy-start(bf16[16,128,256]{2,1,0:T(8,128)(2,1)S(1)} %constant_dynamic-update-slice_fusion.16.own2) | copy-start | bytes 3145732
  65.8 8.2 %collective-permute-start.11 = (bf16[16,128,256]{2,1,0:T(8,128)(2,1)S(1)}, bf16[16,128,256]{2,1,0:T(8,128)(2,1)S(1)}, u32[]{:S(2)}, u32[]{:S(2)}) collective-permute-start(bf16[16,128,256]{2,1,0:T(8,128)(2,1)S(1)} %constant_dynamic-update-slice_fusion.16.own2), channel_id=1, source_target_pairs={{0,1},{1,0},{2,3},{3,2},{4,5},{5,4},{6,7},{7,6},{8,9},{9,8},{10,11... | collective-permute-start | bytes 3145736 | tf_op jit(solution)/shard_map/ppermute | solution.py:466
  66.6 7.4 %copy-start.5 = (bf16[16,288,128]{2,1,0:T(8,128)(2,1)}, bf16[16,288,128]{2,1,0:T(8,128)(2,1)S(1)}, u32[]{:S(2)}) copy-start(bf16[16,288,128]{2,1,0:T(8,128)(2,1)S(1)} %collective-permute-done.5.other.other1) | copy-start | bytes 3538948
  66.6 8.8 %copy-start.6 = (bf16[1,392,512]{2,1,0:T(8,128)(2,1)S(1)}, bf16[1,392,512]{2,1,0:T(8,128)(2,1)}, u32[]{:S(2)}) copy-start(bf16[1,392,512]{2,1,0:T(8,128)(2,1)} %param.16) | copy-start | bytes 1204228
  66.6 8.7 %copy-start.9 = (bf16[392,512]{1,0:T(8,128)(2,1)S(1)}, bf16[392,512]{1,0:T(8,128)(2,1)}, u32[]{:S(2)}) copy-start(bf16[392,512]{1,0:T(8,128)(2,1)} %constant.32.clone.back) | copy-start | bytes 1204228
  74.0 1.0 copy-start.18
  74.0 1.3 copy-start.19
  92.9 1.0 copy-start.12
  108.6 1.5 collective-permute-start.18
  110.2 4.3 %collective-permute-start.19 = (f32[8,16,128]{2,1,0:T(8,128)S(1)}, f32[8,16,128]{2,1,0:T(8,128)S(1)}, u32[]{:S(2)}, u32[]{:S(2)}) collective-permute-start(f32[8,16,128]{2,1,0:T(8,128)S(1)} %slice.189), channel_id=1, source_target_pairs={{0,4},{1,3},{2,6},{3,1},{4,0},{5,7},{6,2},{7,5},{8,12},{9,11},{10,... | collective-permute-start | bytes 196616 | tf_op jit(solution)/shard_map/ppermute | solution.py:466
  114.5 4.0 %collective-permute-start.20 = (f32[4,16,128]{2,1,0:T(8,128)S(1)}, f32[4,16,128]{2,1,0:T(8,128)S(1)}, u32[]{:S(2)}, u32[]{:S(2)}) collective-permute-start(f32[4,16,128]{2,1,0:T(8,128)S(1)} %slice.191), channel_id=1, source_target_pairs={{0,2},{1,5},{2,0},{3,7},{4,6},{5,1},{6,4},{7,3},{8,10},{9,13},{10,... | collective-permute-start | bytes 98312 | tf_op jit(solution)/shard_map/ppermute | solution.py:466
  116.1 22.4 %collective-permute-start.42 = (bf16[16,128,256]{2,1,0:T(8,128)(2,1)}, bf16[16,128,256]{2,1,0:T(8,128)(2,1)}, u32[]{:S(2)}, u32[]{:S(2)}) collective-permute-start(bf16[16,128,256]{2,1,0:T(8,128)(2,1)} %get-tuple-element.55), channel_id=1, source_target_pairs={{0,1},{1,0},{2,3},{3,2},{4,5},{5,4},{6,7},{7,6},{8,9},{9,8},{10,11... | collective-permute-start | bytes 3145736 | tf_op jit(solution)/shard_map/ppermute | solution.py:466
  116.1 27.5 %collective-permute-start.36 = (bf16[16,128,256]{2,1,0:T(8,128)(2,1)S(1)}, bf16[16,128,256]{2,1,0:T(8,128)(2,1)}, u32[]{:S(2)}, u32[]{:S(2)}) collective-permute-start(bf16[16,128,256]{2,1,0:T(8,128)(2,1)S(1)} %get-tuple-element.53), channel_id=1, source_target_pairs={{0,1},{1,0},{2,3},{3,2},{4,5},{5,4},{6,7},{7,6},{8,9},{9,8},{10,11... | collective-permute-start | bytes 3145736 | tf_op jit(solution)/shard_map/ppermute | solution.py:466
  116.6 4.2 %collective-permute-start.30 = (bf16[16,64,128]{2,1,0:T(8,128)(2,1)S(1)}, bf16[16,64,128]{2,1,0:T(8,128)(2,1)S(1)}, u32[]{:S(2)}, u32[]{:S(2)}) collective-permute-start(bf16[16,64,128]{2,1,0:T(8,128)(2,1)S(1)} %get-tuple-element.51), channel_id=1, source_target_pairs={{0,1},{1,0},{2,3},{3,2},{4,5},{5,4},{6,7},{7,6},{8,9},{9,8},{10,11... | collective-permute-start | bytes 786440 | tf_op jit(solution)/shard_map/ppermute | solution.py:466
  118.5 4.6 %collective-permute-start.21 = (f32[16,128]{1,0:T(8,128)S(1)}, f32[16,128]{1,0:T(8,128)S(1)}, u32[]{:S(2)}, u32[]{:S(2)}) collective-permute-start(f32[16,128]{1,0:T(8,128)S(1)} %get-tuple-element.108), channel_id=1, source_target_pairs={{0,8},{1,9},{2,10},{3,11},{4,12},{5,13},{6,14},{7,15},{8,0},{9,1},... | collective-permute-start | bytes 24584 | tf_op jit(solution)/shard_map/ppermute | solution.py:466
  118.6 4.6 %collective-permute-start.22 = (f32[16,128]{1,0:T(8,128)S(1)}, f32[16,128]{1,0:T(8,128)S(1)}, u32[]{:S(2)}, u32[]{:S(2)}) collective-permute-start(f32[16,128]{1,0:T(8,128)S(1)} %get-tuple-element.110), channel_id=1, source_target_pairs={{0,16},{1,17},{2,18},{3,19},{4,20},{5,21},{6,22},{7,23},{8,24},{9,... | collective-permute-start | bytes 24584 | tf_op jit(solution)/shard_map/ppermute | solution.py:466
  120.8 5.4 %collective-permute-start.23 = (f32[16,128]{1,0:T(8,128)S(1)}, f32[16,128]{1,0:T(8,128)S(1)}, u32[]{:S(2)}, u32[]{:S(2)}) collective-permute-start(f32[16,128]{1,0:T(8,128)S(1)} %get-tuple-element.109), channel_id=1, source_target_pairs={{0,24},{1,25},{2,26},{3,27},{4,28},{5,29},{6,30},{7,31},{8,16},{9,... | collective-permute-start | bytes 24584 | tf_op jit(solution)/shard_map/ppermute | solution.py:466
  123.1 9.5 %collective-permute-start.24 = (bf16[16,192,128]{2,1,0:T(8,128)(2,1)S(1)}, bf16[16,192,128]{2,1,0:T(8,128)(2,1)}, u32[]{:S(2)}, u32[]{:S(2)}) collective-permute-start(bf16[16,192,128]{2,1,0:T(8,128)(2,1)S(1)} %get-tuple-element.49), channel_id=1, source_target_pairs={{0,1},{1,0},{2,3},{3,2},{4,5},{5,4},{6,7},{7,6},{8,9},{9,8},{10,11... | collective-permute-start | bytes 2359304 | tf_op jit(solution)/shard_map/ppermute | solution.py:466
  123.2 5.0 %collective-permute-start.31 = (bf16[8,64,128]{2,1,0:T(8,128)(2,1)S(1)}, bf16[8,64,128]{2,1,0:T(8,128)(2,1)S(1)}, u32[]{:S(2)}, u32[]{:S(2)}) collective-permute-start(bf16[8,64,128]{2,1,0:T(8,128)(2,1)S(1)} %slice.209), channel_id=1, source_target_pairs={{0,4},{1,3},{2,6},{3,1},{4,0},{5,7},{6,2},{7,5},{8,12},{9,11},{10,... | collective-permute-start | bytes 393224 | tf_op jit(solution)/shard_map/ppermute | solution.py:466
  128.3 4.3 %collective-permute-start.32 = (bf16[4,64,128]{2,1,0:T(8,128)(2,1)S(1)}, bf16[4,64,128]{2,1,0:T(8,128)(2,1)S(1)}, u32[]{:S(2)}, u32[]{:S(2)}) collective-permute-start(bf16[4,64,128]{2,1,0:T(8,128)(2,1)S(1)} %slice.211), channel_id=1, source_target_pairs={{0,2},{1,5},{2,0},{3,7},{4,6},{5,1},{6,4},{7,3},{8,10},{9,13},{10,... | collective-permute-start | bytes 196616 | tf_op jit(solution)/shard_map/ppermute | solution.py:466
  132.6 8.3 %copy-start.14 = (bf16[16,128,256]{2,1,0:T(8,128)(2,1)S(1)}, bf16[16,128,256]{2,1,0:T(8,128)(2,1)}, u32[]{:S(2)}) copy-start(bf16[16,128,256]{2,1,0:T(8,128)(2,1)} %get-tuple-element.54) | copy-start | bytes 3145732
  134.1 8.4 %collective-permute-start.25 = (bf16[8,192,128]{2,1,0:T(8,128)(2,1)S(1)}, bf16[8,192,128]{2,1,0:T(8,128)(2,1)S(1)}, u32[]{:S(2)}, u32[]{:S(2)}) collective-permute-start(bf16[8,192,128]{2,1,0:T(8,128)(2,1)S(1)} %slice.198), channel_id=1, source_target_pairs={{0,4},{1,3},{2,6},{3,1},{4,0},{5,7},{6,2},{7,5},{8,12},{9,11},{10,... | collective-permute-start | bytes 1179656 | tf_op jit(solution)/shard_map/ppermute | solution.py:466
  135.7 17.0 %collective-permute-start.33 = (bf16[64,128]{1,0:T(8,128)(2,1)S(1)}, bf16[64,128]{1,0:T(8,128)(2,1)S(1)}, u32[]{:S(2)}, u32[]{:S(2)}) collective-permute-start(bf16[64,128]{1,0:T(8,128)(2,1)S(1)} %get-tuple-element.89), channel_id=1, source_target_pairs={{0,8},{1,9},{2,10},{3,11},{4,12},{5,13},{6,14},{7,15},{8,0},{9,1},... | collective-permute-start | bytes 49160 | tf_op jit(solution)/shard_map/ppermute | solution.py:466
  138.5 18.1 %collective-permute-start.34 = (bf16[64,128]{1,0:T(8,128)(2,1)S(1)}, bf16[64,128]{1,0:T(8,128)(2,1)S(1)}, u32[]{:S(2)}, u32[]{:S(2)}) collective-permute-start(bf16[64,128]{1,0:T(8,128)(2,1)S(1)} %get-tuple-element.91), channel_id=1, source_target_pairs={{0,16},{1,17},{2,18},{3,19},{4,20},{5,21},{6,22},{7,23},{8,24},{9,... | collective-permute-start | bytes 49160 | tf_op jit(solution)/shard_map/ppermute | solution.py:466
  138.5 18.1 %collective-permute-start.35 = (bf16[64,128]{1,0:T(8,128)(2,1)S(1)}, bf16[64,128]{1,0:T(8,128)(2,1)S(1)}, u32[]{:S(2)}, u32[]{:S(2)}) collective-permute-start(bf16[64,128]{1,0:T(8,128)(2,1)S(1)} %get-tuple-element.90), channel_id=1, source_target_pairs={{0,24},{1,25},{2,26},{3,27},{4,28},{5,29},{6,30},{7,31},{8,16},{9,... | collective-permute-start | bytes 49160 | tf_op jit(solution)/shard_map/ppermute | solution.py:466
  142.5 2.7 %copy-start.13 = (bf16[16,128,256]{2,1,0:T(8,128)(2,1)S(1)}, bf16[16,128,256]{2,1,0:T(8,128)(2,1)}, u32[]{:S(2)}) copy-start(bf16[16,128,256]{2,1,0:T(8,128)(2,1)} %get-tuple-element.52) | copy-start | bytes 3145732
  142.5 20.8 %collective-permute-start.43 = (bf16[8,128,256]{2,1,0:T(8,128)(2,1)S(1)}, bf16[8,128,256]{2,1,0:T(8,128)(2,1)S(1)}, u32[]{:S(2)}, u32[]{:S(2)}) collective-permute-start(bf16[8,128,256]{2,1,0:T(8,128)(2,1)S(1)} %slice.226), channel_id=1, source_target_pairs={{0,4},{1,3},{2,6},{3,1},{4,0},{5,7},{6,2},{7,5},{8,12},{9,11},{10,... | collective-permute-start | bytes 1572872 | tf_op jit(solution)/shard_map/ppermute | solution.py:466
  143.6 7.8 %collective-permute-start.26 = (bf16[4,192,128]{2,1,0:T(8,128)(2,1)S(1)}, bf16[4,192,128]{2,1,0:T(8,128)(2,1)S(1)}, u32[]{:S(2)}, u32[]{:S(2)}) collective-permute-start(bf16[4,192,128]{2,1,0:T(8,128)(2,1)S(1)} %slice.200), channel_id=1, source_target_pairs={{0,2},{1,5},{2,0},{3,7},{4,6},{5,1},{6,4},{7,3},{8,10},{9,13},{10,... | collective-permute-start | bytes 589832 | tf_op jit(solution)/shard_map/ppermute | solution.py:466
  151.5 14.1 %collective-permute-start.37 = (bf16[8,128,256]{2,1,0:T(8,128)(2,1)S(1)}, bf16[8,128,256]{2,1,0:T(8,128)(2,1)S(1)}, u32[]{:S(2)}, u32[]{:S(2)}) collective-permute-start(bf16[8,128,256]{2,1,0:T(8,128)(2,1)S(1)} %slice.217), channel_id=1, source_target_pairs={{0,4},{1,3},{2,6},{3,1},{4,0},{5,7},{6,2},{7,5},{8,12},{9,11},{10,... | collective-permute-start | bytes 1572872 | tf_op jit(solution)/shard_map/ppermute | solution.py:466
  152.7 7.0 %collective-permute-start.27 = (bf16[192,128]{1,0:T(8,128)(2,1)S(1)}, bf16[192,128]{1,0:T(8,128)(2,1)S(1)}, u32[]{:S(2)}, u32[]{:S(2)}) collective-permute-start(bf16[192,128]{1,0:T(8,128)(2,1)S(1)} %get-tuple-element.78), channel_id=1, source_target_pairs={{0,8},{1,9},{2,10},{3,11},{4,12},{5,13},{6,14},{7,15},{8,0},{9,1},... | collective-permute-start | bytes 147464 | tf_op jit(solution)/shard_map/ppermute | solution.py:466
  156.6 5.0 %collective-permute-start.28 = (bf16[192,128]{1,0:T(8,128)(2,1)S(1)}, bf16[192,128]{1,0:T(8,128)(2,1)S(1)}, u32[]{:S(2)}, u32[]{:S(2)}) collective-permute-start(bf16[192,128]{1,0:T(8,128)(2,1)S(1)} %get-tuple-element.80), channel_id=1, source_target_pairs={{0,16},{1,17},{2,18},{3,19},{4,20},{5,21},{6,22},{7,23},{8,24},{9,... | collective-permute-start | bytes 147464 | tf_op jit(solution)/shard_map/ppermute | solution.py:466
  156.6 6.1 %collective-permute-start.29 = (bf16[192,128]{1,0:T(8,128)(2,1)S(1)}, bf16[192,128]{1,0:T(8,128)(2,1)S(1)}, u32[]{:S(2)}, u32[]{:S(2)}) collective-permute-start(bf16[192,128]{1,0:T(8,128)(2,1)S(1)} %get-tuple-element.79), channel_id=1, source_target_pairs={{0,24},{1,25},{2,26},{3,27},{4,28},{5,29},{6,30},{7,31},{8,16},{9,... | collective-permute-start | bytes 147464 | tf_op jit(solution)/shard_map/ppermute | solution.py:466
  163.5 6.4 %collective-permute-start.44 = (bf16[4,128,256]{2,1,0:T(8,128)(2,1)S(1)}, bf16[4,128,256]{2,1,0:T(8,128)(2,1)S(1)}, u32[]{:S(2)}, u32[]{:S(2)}) collective-permute-start(bf16[4,128,256]{2,1,0:T(8,128)(2,1)S(1)} %slice.228), channel_id=1, source_target_pairs={{0,2},{1,5},{2,0},{3,7},{4,6},{5,1},{6,4},{7,3},{8,10},{9,13},{10,... | collective-permute-start | bytes 786440 | tf_op jit(solution)/shard_map/ppermute | solution.py:466
  165.8 8.7 %collective-permute-start.38 = (bf16[4,128,256]{2,1,0:T(8,128)(2,1)S(1)}, bf16[4,128,256]{2,1,0:T(8,128)(2,1)S(1)}, u32[]{:S(2)}, u32[]{:S(2)}) collective-permute-start(bf16[4,128,256]{2,1,0:T(8,128)(2,1)S(1)} %slice.219), channel_id=1, source_target_pairs={{0,2},{1,5},{2,0},{3,7},{4,6},{5,1},{6,4},{7,3},{8,10},{9,13},{10,... | collective-permute-start | bytes 786440 | tf_op jit(solution)/shard_map/ppermute | solution.py:466
  170.0 7.6 %collective-permute-start.45 = (bf16[128,256]{1,0:T(8,128)(2,1)S(1)}, bf16[128,256]{1,0:T(8,128)(2,1)S(1)}, u32[]{:S(2)}, u32[]{:S(2)}) collective-permute-start(bf16[128,256]{1,0:T(8,128)(2,1)S(1)} %get-tuple-element.68), channel_id=1, source_target_pairs={{0,8},{1,9},{2,10},{3,11},{4,12},{5,13},{6,14},{7,15},{8,0},{9,1},... | collective-permute-start | bytes 196616 | tf_op jit(solution)/shard_map/ppermute | solution.py:466
  170.7 8.4 %collective-permute-start.46 = (bf16[128,256]{1,0:T(8,128)(2,1)S(1)}, bf16[128,256]{1,0:T(8,128)(2,1)S(1)}, u32[]{:S(2)}, u32[]{:S(2)}) collective-permute-start(bf16[128,256]{1,0:T(8,128)(2,1)S(1)} %get-tuple-element.70), channel_id=1, source_target_pairs={{0,16},{1,17},{2,18},{3,19},{4,20},{5,21},{6,22},{7,23},{8,24},{9,... | collective-permute-start | bytes 196616 | tf_op jit(solution)/shard_map/ppermute | solution.py:466
  173.0 6.2 %collective-permute-start.47 = (bf16[128,256]{1,0:T(8,128)(2,1)S(1)}, bf16[128,256]{1,0:T(8,128)(2,1)S(1)}, u32[]{:S(2)}, u32[]{:S(2)}) collective-permute-start(bf16[128,256]{1,0:T(8,128)(2,1)S(1)} %get-tuple-element.69), channel_id=1, source_target_pairs={{0,24},{1,25},{2,26},{3,27},{4,28},{5,29},{6,30},{7,31},{8,16},{9,... | collective-permute-start | bytes 196616 | tf_op jit(solution)/shard_map/ppermute | solution.py:466
  174.6 5.4 %collective-permute-start.39 = (bf16[128,256]{1,0:T(8,128)(2,1)S(1)}, bf16[128,256]{1,0:T(8,128)(2,1)S(1)}, u32[]{:S(2)}, u32[]{:S(2)}) collective-permute-start(bf16[128,256]{1,0:T(8,128)(2,1)S(1)} %get-tuple-element.71), channel_id=1, source_target_pairs={{0,8},{1,9},{2,10},{3,11},{4,12},{5,13},{6,14},{7,15},{8,0},{9,1},... | collective-permute-start | bytes 196616 | tf_op jit(solution)/shard_map/ppermute | solution.py:466
  175.3 5.2 %collective-permute-start.40 = (bf16[128,256]{1,0:T(8,128)(2,1)S(1)}, bf16[128,256]{1,0:T(8,128)(2,1)S(1)}, u32[]{:S(2)}, u32[]{:S(2)}) collective-permute-start(bf16[128,256]{1,0:T(8,128)(2,1)S(1)} %get-tuple-element.73), channel_id=1, source_target_pairs={{0,16},{1,17},{2,18},{3,19},{4,20},{5,21},{6,22},{7,23},{8,24},{9,... | collective-permute-start | bytes 196616 | tf_op jit(solution)/shard_map/ppermute | solution.py:466
  177.6 6.1 %collective-permute-start.41 = (bf16[128,256]{1,0:T(8,128)(2,1)S(1)}, bf16[128,256]{1,0:T(8,128)(2,1)S(1)}, u32[]{:S(2)}, u32[]{:S(2)}) collective-permute-start(bf16[128,256]{1,0:T(8,128)(2,1)S(1)} %get-tuple-element.72), channel_id=1, source_target_pairs={{0,24},{1,25},{2,26},{3,27},{4,28},{5,29},{6,30},{7,31},{8,16},{9,... | collective-permute-start | bytes 196616 | tf_op jit(solution)/shard_map/ppermute | solution.py:466
  (4 other events, 2.7 us)
